TPU v7x, 128 devices: a whole 4x4x4 slice. The times are simulated.
128 devices in a mesh: blk: 128 (over x, y, z, core).
Axes of the slice: x: 4, y: 4, z: 4, core: 2. Of those that a mesh axis runs over, the one named last changes fastest.
Arguments:
- adjoint: float32 [128, 19, 4096], P('blk'), may hold values from -6 to 6
- velocity: float32 [128, 3, 4096], P('blk'), may hold values from -0.15 to 0.15
- relax: float32 [128, 4096], P('blk'), may hold values from 0.6 to 1.9
- fluid_words: int32 [128, 128], P('blk'), may hold values from -2147483648 to 2147483647, as said below
- neighbours: int32 [128, 18], P('blk'), may hold values from -1 to 127, as said below
- inlet_ids: int32 [16], replicated, may hold values from 0 to 127, as said below
- basis: float32 [8, 16, 256], replicated, may hold values from -0.09375 to 0.09375
Outputs:
- adjoint_prev: float32 [128, 19, 4096], P('blk')
- inlet_grad: float32 [8], replicated
Inputs may be any that keep to these rules, and one draw needn't show every extreme that they name: `neighbours`: entry k of a block's row names, as device + slot, the occupied block holding the sites beyond it along the velocity of index k + 1 (entries 0 to 5 faces, 6 to 17 edges), or is -1 where there is none; the named block's device is at most 2 indices from the block's device, and in every draw some block names blocks exactly 2 devices away on both sides. Every device holds one occupied block. `fluid_words`: unoccupied slots have no fluid sites. `inlet_ids`: 16 distinct occupied blocks, as device + slot.
All inputs are finite; a program needn't handle non-finite values.
Results may differ from a plain program's by a relative error of at most 0.0003.
Values sent between devices are 32-bit elements; how exact they have to be, the bound alone decides.
A program may use at most 128 MiB of HBM per device.

v0:
```python
import jax
import jax.numpy as jnp
import numpy as np
from jax import lax
from jax.experimental import pallas as pl
from jax.experimental.pallas import tpu as pltpu
from jax.sharding import PartitionSpec as P

EDGE = 16
VELS = 19
NEIGHBOURS = 18
REACH = 2
STEPS = 4
LANES = 128
NIN = 16
MODES = 8

C = np.array(
    [
        [0, 0, 0],
        [1, 0, 0],
        [-1, 0, 0],
        [0, 1, 0],
        [0, -1, 0],
        [0, 0, 1],
        [0, 0, -1],
        [1, 1, 0],
        [-1, -1, 0],
        [1, -1, 0],
        [-1, 1, 0],
        [1, 0, 1],
        [-1, 0, -1],
        [1, 0, -1],
        [-1, 0, 1],
        [0, 1, 1],
        [0, -1, -1],
        [0, 1, -1],
        [0, -1, 1],
    ],
    dtype=np.int32,
)
OPP = [0, 2, 1, 4, 3, 6, 5, 8, 7, 10, 9, 12, 11, 14, 13, 16, 15, 18, 17]
DIRECTION = {tuple(int(v) for v in C[k + 1]): k for k in range(NEIGHBOURS)}

FLUID = -1
MEMBERS = {
    (axis, sign): [i for i in range(VELS) if C[i][axis] == sign] + [FLUID]
    for axis in range(3)
    for sign in (1, -1)
}
X_BASE = {1: 0, -1: 12}
Y_BASE = {1: 24, -1: 40}
Z_BASE = 56
ROWS = 88
OWN = REACH


def z_slot(sign, item):
    return MEMBERS[(2, sign)].index(item) + (0 if sign == 1 else 6)


def lane_roll(value, by):
    by = by % LANES
    return value if by == 0 else pltpu.roll(value, LANES - by, 1)


def row_roll(value, by):
    return pltpu.roll(value, (-by) % EDGE, 0)


class Masks:
    def __init__(self):
        self.lane = lax.broadcasted_iota(jnp.int32, (EDGE, LANES), 1)
        self.row = lax.broadcasted_iota(jnp.int32, (EDGE, LANES), 0)
        self.z = self.lane % EDGE
        self.yl = self.lane // EDGE


def pack(package, load, plane_row, items, masks):
    for sign in (1, -1):
        x_at = 0 if sign == 1 else EDGE - 1
        for slot, item in enumerate(MEMBERS[(0, sign)]):
            if item in items:
                for yh in range(2):
                    package[pl.ds(X_BASE[sign] + 2 * slot + yh, 1), :] = plane_row(item, yh, x_at)
    for sign in (1, -1):
        yh, start = (0, 0) if sign == 1 else (1, LANES - EDGE)
        block = None
        for slot, item in enumerate(MEMBERS[(1, sign)]):
            if item in items:
                moved = lane_roll(load(item, yh), start - slot * EDGE)
                block = moved if block is None else jnp.where(masks.yl == slot, moved, block)
        package[pl.ds(Y_BASE[sign], EDGE), :] = block
    for yh in range(2):
        block = None
        for sign in (1, -1):
            start = 0 if sign == 1 else EDGE - 1
            for item in MEMBERS[(2, sign)]:
                if item in items:
                    slot = z_slot(sign, item)
                    moved = lane_roll(load(item, yh), start - slot)
                    block = moved if block is None else jnp.where(masks.z == slot, moved, block)
        package[pl.ds(Z_BASE + yh * EDGE, EDGE), :] = block


def pull(field, item, c, ghost, masks):
    cx, cy, cz = (int(v) for v in c)
    v0, v1 = field
    if cx:
        edge = masks.row == (EDGE - 1 if cx == 1 else 0)
        base = X_BASE[cx] + 2 * MEMBERS[(0, cx)].index(item)
        v0 = jnp.where(edge, ghost((cx, 0, 0), base, 1), row_roll(v0, cx))
        v1 = jnp.where(edge, ghost((cx, 0, 0), base + 1, 1), row_roll(v1, cx))
    if cy:
        slot = MEMBERS[(1, cy)].index(item)
        at = 0 if cy == 1 else LANES - EDGE
        plane = lane_roll(ghost((0, cy, 0), Y_BASE[cy], EDGE), slot * EDGE - at)
        if cx:
            line = ghost((cx, cy, 0), base + (0 if cy == 1 else 1), 1)
            plane = jnp.where(edge, line, row_roll(plane, cx))
        if cy == 1:
            take = masks.lane < EDGE
            v0, v1 = jnp.where(take, v1, v0), jnp.where(take, plane, v1)
        else:
            take = masks.lane >= LANES - EDGE
            v0, v1 = jnp.where(take, plane, v0), jnp.where(take, v0, v1)
        v0, v1 = lane_roll(v0, cy * EDGE), lane_roll(v1, cy * EDGE)
    if cz:
        target = EDGE - 1 if cz == 1 else 0
        slot = z_slot(cz, item)
        g = [lane_roll(ghost((0, 0, cz), Z_BASE + yh * EDGE, EDGE), slot - target) for yh in range(2)]
        source = EDGE - 1 - target
        if cx:
            for yh in range(2):
                line = lane_roll(ghost((cx, 0, cz), base + yh, 1), source - target)
                g[yh] = jnp.where(edge, line, row_roll(g[yh], cx))
        if cy:
            line = lane_roll(
                ghost((0, cy, cz), Y_BASE[cy], EDGE),
                MEMBERS[(1, cy)].index(item) * EDGE + source - (at + target),
            )
            if cy == 1:
                g = [jnp.where(take, g[1], g[0]), jnp.where(take, line, g[1])]
            else:
                g = [jnp.where(take, line, g[0]), jnp.where(take, g[0], g[1])]
            g = [lane_roll(v, cy * EDGE) for v in g]
        here = masks.z == target
        v0 = jnp.where(here, g[0], lane_roll(v0, cz))
        v1 = jnp.where(here, g[1], lane_roll(v1, cz))
    return v0, v1


def collide(b, u, k, g, e):
    ux, uy, uz = u
    pairs = [(i, i + 1) for i in range(1, VELS, 2)]
    s = {i: b[i] + b[j] for i, j in pairs}
    d = {i: b[i] - b[j] for i, j in pairs}
    p, q, r = s[7] + s[9], s[11] + s[13], s[15] + s[17]
    sx, sy, sz = s[1] + s[1], s[3] + s[3], s[5] + s[5]
    mxx, myy, mzz = sx + (p + q), sy + (p + r), sz + (q + r)
    mxy, mxz, myz = s[7] - s[9], s[11] - s[13], s[15] - s[17]
    m0 = 12.0 * b[0] + (sx + sy + sz) + (p + q + r)
    m1x = (d[1] + d[1]) + (d[7] + d[9]) + (d[11] + d[13])
    m1y = (d[3] + d[3]) + (d[7] - d[9]) + (d[15] + d[17])
    m1z = (d[5] + d[5]) + (d[11] - d[13]) + (d[15] - d[17])
    nx = mxx * ux + mxy * uy + mxz * uz
    ny = mxy * ux + myy * uy + myz * uz
    nz = mxz * ux + myz * uy + mzz * uz
    vx = g * (m1x + 3.0 * nx - ux * m0)
    vy = g * (m1y + 3.0 * ny - uy * m0)
    vz = g * (m1z + 3.0 * nz - uz * m0)
    o = g * (m0 * e - 1.5 * (ux * nx + uy * ny + uz * nz))
    v = {1: vx, 3: vy, 5: vz, 7: vx + vy, 9: vx - vy, 11: vx + vz, 13: vx - vz, 15: vy + vz, 17: vy - vz}
    out = [k * b[0] + o]
    for i, j in pairs:
        out.append(k * b[i] + (o + v[i]))
        out.append(k * b[j] + (o - v[i]))
    return out


def body(n, inner, *refs):
    (a_hbm, vel_hbm, relax_hbm, words, nbrs, ids, basis_hbm) = refs[:7]
    (out_hbm, grad) = refs[7:9]
    (a, b, vel, relax, basis, fluid, bits, coef) = refs[9:17]
    bufs = refs[17 : 17 + STEPS]
    (part1, part2, local_sem, send_sem, recv_sem, sum_send1, sum_recv1, sum_send2, sum_recv2) = refs[17 + STEPS :]
    me = lax.axis_index("blk")
    outer = n // inner
    place = me % inner
    group = me // inner
    offsets = (2, -2, 1, -1)
    halo_peers = [(me + d + n) % n for d in offsets]
    inner_peers = [group * inner + (place + j) % inner for j in range(1, inner)]
    outer_peers = [((group + j) % outer) * inner + place for j in range(1, outer)]
    peers = halo_peers + inner_peers + outer_peers

    barrier = pltpu.get_barrier_semaphore()
    for peer in peers:
        pl.semaphore_signal(barrier, inc=1, device_id=(peer,), device_id_type=pl.DeviceIdType.MESH)

    loads = []
    for yh in range(2):
        loads.append(pltpu.make_async_copy(a_hbm.at[:, :, yh, :], a.at[:, yh], local_sem.at[yh]))
        loads.append(pltpu.make_async_copy(vel_hbm.at[:, :, yh, :], vel.at[:, yh], local_sem.at[2 + yh]))
        loads.append(pltpu.make_async_copy(relax_hbm.at[:, yh, :], relax.at[yh], local_sem.at[4 + yh]))
    loads.append(pltpu.make_async_copy(basis_hbm, basis, local_sem.at[6]))
    for load in loads:
        load.start()

    masks = Masks()
    for yh in range(2):
        word = jnp.zeros((EDGE, LANES), jnp.int32)
        for x in range(EDGE):
            at = x * 8 + yh * 4
            w = [words[0, at + j] for j in range(4)]
            line = jnp.where(
                masks.lane < 64,
                jnp.where(masks.lane < 32, w[0], w[1]),
                jnp.where(masks.lane < 96, w[2], w[3]),
            )
            word = jnp.where(masks.row == x, line, word)
        bit = jnp.bitwise_and(jnp.right_shift(word, masks.lane % 32), 1)
        fluid[yh] = bit.astype(jnp.float32)

    is_inlet = jnp.int32(0)
    for r in range(NIN):
        is_inlet = is_inlet + (ids[r] == me).astype(jnp.int32)
    keep = 1.0 - is_inlet.astype(jnp.float32)
    keep_z = jnp.where(masks.z == 0, keep, 1.0)
    slot_of = []
    present = []
    for k in range(NEIGHBOURS):
        entry = nbrs[0, k]
        there = (entry >= 0).astype(jnp.int32)
        slot = jnp.clip(entry - me + OWN, 0, 2 * REACH)
        slot_of.append(slot * there + OWN * (1 - there))
        present.append(there.astype(jnp.float32))

    def send(step):
        copies = []
        for index, d in enumerate(offsets):
            copies.append(
                pltpu.make_async_remote_copy(
                    src_ref=bufs[step].at[OWN],
                    dst_ref=bufs[step].at[OWN - d],
                    send_sem=send_sem.at[step, index],
                    recv_sem=recv_sem.at[step, index],
                    device_id=(halo_peers[index],),
                    device_id_type=pl.DeviceIdType.MESH,
                )
            )
        for copy in copies:
            copy.start()
        return copies

    everything = set(range(1, VELS))
    layer = [jnp.zeros((EDGE, LANES), jnp.float32) for _ in range(2)]

    for load in loads:
        load.wait()
    for step in range(STEPS):
        items = everything | ({FLUID} if step == 0 else set())
        pack(
            bufs[step].at[OWN],
            lambda item, yh: fluid[yh] if item == FLUID else a[item, yh],
            lambda item, yh, x: fluid[yh, pl.ds(x, 1), :] if item == FLUID else a[item, yh, pl.ds(x, 1), :],
            items,
            masks,
        )
        if step == 0:
            pl.semaphore_wait(barrier, len(peers))
        copies = send(step)
        for yh in range(2):
            layer[yh] = layer[yh] + (2.0 * a[5, yh] + ((a[11, yh] + a[14, yh]) + (a[15, yh] + a[18, yh])))
            if step == 0:
                f = fluid[yh]
                squared = vel[0, yh] * vel[0, yh] + vel[1, yh] * vel[1, yh] + vel[2, yh] * vel[2, yh]
                coef[0, yh] = f * (1.0 - relax[yh])
                coef[1, yh] = f * relax[yh] * (1.0 / 12.0)
                coef[2, yh] = (1.0 / 3.0) + 0.5 * squared
        if step == STEPS - 1:
            site = lax.broadcasted_iota(jnp.int32, (LANES, 2 * LANES), 0)
            flat = lax.broadcasted_iota(jnp.int32, (LANES, 2 * LANES), 1)
            spread = jnp.zeros((EDGE, 2 * LANES), jnp.float32)
            for yh in range(2):
                pick = ((site % EDGE == 0) & (site // EDGE + 8 * yh == flat % EDGE)).astype(jnp.float32)
                value = jnp.where(masks.z == 0, layer[yh] * fluid[yh], 0.0) * (1.0 / 12.0)
                spread = spread + jnp.dot(
                    value, pick, precision=lax.Precision.HIGHEST, preferred_element_type=jnp.float32
                )
            row = lax.broadcasted_iota(jnp.int32, (EDGE, 2 * LANES), 0)
            lane = lax.broadcasted_iota(jnp.int32, (EDGE, 2 * LANES), 1)
            line = jnp.sum(jnp.where(lane // EDGE == row, spread, 0.0), axis=0, keepdims=True)
            weight = jnp.zeros((EDGE, 2 * LANES), jnp.float32)
            for r in range(NIN):
                mine = (ids[r] == me).astype(jnp.float32)
                weight = jnp.where(row == r, mine, weight)
            weight = weight * line
            mode = lax.broadcasted_iota(jnp.int32, (MODES, LANES), 0)
            total = jnp.zeros((MODES, LANES), jnp.float32)
            for m in range(MODES):
                product = jnp.sum(basis[m] * weight, axis=0, keepdims=True)
                total = jnp.where(mode == m, product[:, :LANES] + product[:, LANES:], total)
            part1[0] = total
            sums1 = []
            for j in range(1, inner):
                sums1.append(
                    pltpu.make_async_remote_copy(
                        src_ref=part1.at[0],
                        dst_ref=part1.at[j],
                        send_sem=sum_send1.at[j - 1],
                        recv_sem=sum_recv1.at[j - 1],
                        device_id=(inner_peers[j - 1],),
                        device_id_type=pl.DeviceIdType.MESH,
                    )
                )
            for copy in sums1:
                copy.start()
            for copy in sums1:
                copy.wait()
            total = part1[0]
            for j in range(1, inner):
                total = total + part1[j]
            part2[0] = total
            sums2 = []
            for j in range(1, outer):
                sums2.append(
                    pltpu.make_async_remote_copy(
                        src_ref=part2.at[0],
                        dst_ref=part2.at[j],
                        send_sem=sum_send2.at[j - 1],
                        recv_sem=sum_recv2.at[j - 1],
                        device_id=(outer_peers[j - 1],),
                        device_id_type=pl.DeviceIdType.MESH,
                    )
                )
            for copy in sums2:
                copy.start()
        for copy in copies:
            copy.wait()

        buf = bufs[step]

        def ghost(direction, row, rows):
            return buf[slot_of[DIRECTION[direction]], pl.ds(row, rows), :]

        if step == 0:

            def ghost_fluid(direction, row, rows):
                k = DIRECTION[direction]
                return buf[slot_of[k], pl.ds(row, rows), :] * present[k]

            for i in range(1, VELS):
                m0, m1 = pull((fluid[0], fluid[1]), FLUID, C[i], ghost_fluid, masks)
                bits[i - 1, 0] = m0
                bits[i - 1, 1] = m1
        for yh in range(2):
            b[0, yh] = a[0, yh]
        for i in range(1, VELS):
            pulled = pull((a[i, 0], a[i, 1]), i, C[i], ghost, masks)
            for yh in range(2):
                value = jnp.where(bits[i - 1, yh] > 0.5, pulled[yh], a[OPP[i], yh])
                if C[i][2] == -1:
                    value = value * keep_z
                b[i, yh] = value
        for yh in range(2):
            for half in range(2):
                rows = pl.ds(8 * half, 8)
                new = collide(
                    [b[i, yh, rows, :] for i in range(VELS)],
                    [vel[c, yh, rows, :] for c in range(3)],
                    coef[0, yh, rows, :],
                    coef[1, yh, rows, :],
                    coef[2, yh, rows, :],
                )
                for i in range(VELS):
                    a[i, yh, rows, :] = new[i]

    stores = [
        pltpu.make_async_copy(a.at[:, yh], out_hbm.at[:, :, yh, :], local_sem.at[yh]) for yh in range(2)
    ]
    for store in stores:
        store.start()
    for copy in sums2:
        copy.wait()
    total = part2[0]
    for j in range(1, outer):
        total = total + part2[j]
    ones = jnp.ones((8, LANES), jnp.float32)
    result = lax.dot_general(
        ones, total, (((1,), (1,)), ((), ())), precision=lax.Precision.HIGHEST, preferred_element_type=jnp.float32
    )
    grad[...] = result[0:1, :]
    for store in stores:
        store.wait()


def on_device(adjoint, velocity, relax, fluid_words, neighbours, inlet_ids, basis):
    n = lax.axis_size("blk")
    inner = 8 if n % 64 == 0 else 4
    outer = n // inner
    f32 = jnp.float32
    shape = (EDGE, 2, LANES)
    any_space = pl.BlockSpec(memory_space=pl.ANY)
    smem = pl.BlockSpec(memory_space=pltpu.SMEM)
    dma = pltpu.SemaphoreType.DMA
    out, grad = pl.pallas_call(
        lambda *refs: body(n, inner, *refs),
        out_shape=(
            jax.ShapeDtypeStruct((VELS,) + shape, f32),
            jax.ShapeDtypeStruct((1, MODES), f32),
        ),
        in_specs=[any_space, any_space, any_space, smem, smem, smem, any_space],
        out_specs=(any_space, pl.BlockSpec(memory_space=pltpu.VMEM)),
        scratch_shapes=[
            pltpu.VMEM((VELS, 2, EDGE, LANES), f32),
            pltpu.VMEM((VELS, 2, EDGE, LANES), f32),
            pltpu.VMEM((3, 2, EDGE, LANES), f32),
            pltpu.VMEM((2, EDGE, LANES), f32),
            pltpu.VMEM((MODES, NIN, 2 * LANES), f32),
            pltpu.VMEM((2, EDGE, LANES), f32),
            pltpu.VMEM((VELS - 1, 2, EDGE, LANES), f32),
            pltpu.VMEM((3, 2, EDGE, LANES), f32),
        ]
        + [pltpu.VMEM((2 * REACH + 1, ROWS, LANES), f32) for _ in range(STEPS)]
        + [
            pltpu.VMEM((inner, MODES, LANES), f32),
            pltpu.VMEM((outer, MODES, LANES), f32),
            dma((7,)),
            dma((STEPS, 4)),
            dma((STEPS, 4)),
            dma((inner - 1,)),
            dma((inner - 1,)),
            dma((outer - 1,)),
            dma((outer - 1,)),
        ],
        compiler_params=pltpu.CompilerParams(collective_id=0, has_side_effects=True),
        name="adjoint_steps",
    )(
        adjoint.reshape((VELS,) + shape),
        velocity.reshape((3,) + shape),
        relax.reshape(shape),
        fluid_words,
        neighbours,
        inlet_ids,
        basis,
    )
    return (out.reshape(1, VELS, EDGE * EDGE * EDGE), grad.reshape(MODES))


def solution(mesh):
    return jax.shard_map(
        on_device,
        mesh=mesh,
        in_specs=(
            P("blk", None, None),
            P("blk", None, None),
            P("blk", None),
            P("blk", None),
            P("blk", None),
            P(),
            P(),
        ),
        out_specs=(P("blk", None, None), P()),
        check_vma=False,
    )
```

profile of v0, /device:TPU:1, one launch (start us, length us, event | category | flops | bytes accessed | tf_op | source)
XLA Modules:
  0.0 42.3 jit_solution(13469345158956855217)
XLA Ops:
  0.6 39.4 %adjoint_steps.1 = (f32[19,16,2,128]{3,2,1,0:T(2,128)}, f32[1,8]{1,0:T(1,128)}) custom-call(f32[19,16,2,128]{3,2,1,0:T(2,128)} %bitcast.5, f32[3,16,2,128]{3,2,1,0:T(2,128)} %bitcast.7, f32[16,2,128]{2,1,0:T(2,128)} %bitcast.8, s32[1,128]{1,0:T(1,128)} %refs_3_.1, s32[1,18]{1,0:T(1,128)} %refs_4_.1, s32[16]{0:T(128)} %refs_5_.1, f32[8,16,256]{2,1,0:T(8,128)} %refs_6_.1), custom_call_target="tpu_custom_call" | custom-call | tf_op jit(solution)/shard_map/adjoint_steps/pallas_call | solution.py:407
  40.1 0.0 copy-start
  40.1 1.7 %copy.13 = f32[1,19,4096]{2,0,1:T(1,128)} copy(f32[1,19,4096]{2,0,1:T(1,128)} %bitcast.6) | data formatting | bytes 622592
  41.8 0.0 copy-done
  41.8 0.5 %copy.14 = f32[8]{0:T(128)} copy(f32[8]{0:T(128)S(1)} %bitcast.9) | data formatting | bytes 64
Async XLA Ops:
  40.1 1.7 %copy-start = (f32[1,8]{1,0:T(1,128)S(1)}, f32[1,8]{1,0:T(1,128)}, u32[]{:S(2)}) copy-start(f32[1,8]{1,0:T(1,128)} %get-tuple-element.5) | copy-start | bytes 100
where the time goes:
time: 42.5 us; the launch traced here: 42.3 us
  Pallas kernels  39.4 us (93%)
  local copies, waits for them, and re-layouts  2.22 us (5%)
  between operations  0.65 us (2%)
    pallas_call x1, Pallas kernels, on_device(): pl.pallas_call(lambda *refs: body(n, inner, *refs), out_shape=(jax.ShapeD...  39.4 us
    unnamed x4, local copies, waits for them, and re-layouts  2.22 us

commit v1 on v0

--- a/solution.py
+++ b/solution.py
@@ -43,20 +43,31 @@
 DIRECTION = {tuple(int(v) for v in C[k + 1]): k for k in range(NEIGHBOURS)}
 
 FLUID = -1
-MEMBERS = {
-    (axis, sign): [i for i in range(VELS) if C[i][axis] == sign] + [FLUID]
-    for axis in range(3)
-    for sign in (1, -1)
-}
-X_BASE = {1: 0, -1: 12}
-Y_BASE = {1: 24, -1: 40}
-Z_BASE = 56
-ROWS = 88
+
+
+def members(axis, sign):
+    found = [i for i in range(VELS) if C[i][axis] == sign]
+    return sorted(found, key=lambda i: int(np.abs(C[i]).sum()), reverse=True)
+
+
+Z_ROWS, Y_ROWS, AXIS_ROWS, X_ROWS, X_FLUID, YZ_FLUID = 0, 16, 32, 48, 68, 72
+SENT, ROWS = 68, 88
+SIGNS = (1, -1)
+Z_NUMBER = {i: n for n, i in enumerate([i for s in SIGNS for i in members(2, s)[:4]])}
+Y_NUMBER = {i: n for n, i in enumerate([i for s in SIGNS for i in members(1, s)[:4]])}
+X_NUMBER = {i: n for n, i in enumerate([i for s in SIGNS for i in members(0, s)])}
+CUT = 12
 OWN = REACH
 
 
-def z_slot(sign, item):
-    return MEMBERS[(2, sign)].index(item) + (0 if sign == 1 else 6)
+def sign_index(sign):
+    return 0 if sign == 1 else 1
+
+
+def x_row(item, sign, yh):
+    if item == FLUID:
+        return X_FLUID + 2 * sign_index(sign) + yh
+    return X_ROWS + 2 * X_NUMBER[item] + yh
 
 
 def lane_roll(value, by):
@@ -76,31 +87,78 @@
         self.yl = self.lane // EDGE
 
 
-def pack(package, load, plane_row, items, masks):
-    for sign in (1, -1):
+def put(block, mask, value):
+    return value if block is None else jnp.where(mask, value, block)
+
+
+def pack_axis(load, items, masks):
+    block = None
+    for sign in SIGNS:
+        yh, start = (0, 0) if sign == 1 else (1, LANES - EDGE)
+        plane = load(items[(1, sign)], yh)
+        at = 4 * sign_index(sign) * EDGE + 4
+        first = lane_roll(plane, start - at)
+        second = lane_roll(plane, start + CUT - at - EDGE)
+        block = put(block, masks.yl == at // EDGE, first)
+        block = put(block, masks.yl == at // EDGE + 1, second)
+    for sign in SIGNS:
+        start = 0 if sign == 1 else EDGE - 1
+        for yh in range(2):
+            slot = 2 * sign_index(sign) + yh
+            block = put(block, masks.z == slot, lane_roll(load(items[(2, sign)], yh), start - slot))
+    return block
+
+
+def pack(package, a, fluid, masks):
+    def load(item, yh):
+        return fluid[yh] if item == FLUID else a[item, yh]
+
+    block = None
+    for sign in SIGNS:
+        start = 0 if sign == 1 else EDGE - 1
+        for item in members(2, sign)[:4]:
+            for yh in range(2):
+                slot = 2 * Z_NUMBER[item] + yh
+                block = put(block, masks.z == slot, lane_roll(load(item, yh), start - slot))
+    package[pl.ds(Z_ROWS, EDGE), :] = block
+    block = None
+    for sign in SIGNS:
+        yh, start = (0, 0) if sign == 1 else (1, LANES - EDGE)
+        for item in members(1, sign)[:4]:
+            number = Y_NUMBER[item]
+            block = put(block, masks.yl == number, lane_roll(load(item, yh), start - number * EDGE))
+    package[pl.ds(Y_ROWS, EDGE), :] = block
+    axis = {(1, 1): 3, (1, -1): 4, (2, 1): 5, (2, -1): 6}
+    package[pl.ds(AXIS_ROWS, EDGE), :] = pack_axis(load, axis, masks)
+    for sign in SIGNS:
         x_at = 0 if sign == 1 else EDGE - 1
-        for slot, item in enumerate(MEMBERS[(0, sign)]):
-            if item in items:
-                for yh in range(2):
-                    package[pl.ds(X_BASE[sign] + 2 * slot + yh, 1), :] = plane_row(item, yh, x_at)
-    for sign in (1, -1):
-        yh, start = (0, 0) if sign == 1 else (1, LANES - EDGE)
-        block = None
-        for slot, item in enumerate(MEMBERS[(1, sign)]):
-            if item in items:
-                moved = lane_roll(load(item, yh), start - slot * EDGE)
-                block = moved if block is None else jnp.where(masks.yl == slot, moved, block)
-        package[pl.ds(Y_BASE[sign], EDGE), :] = block
-    for yh in range(2):
-        block = None
-        for sign in (1, -1):
-            start = 0 if sign == 1 else EDGE - 1
-            for item in MEMBERS[(2, sign)]:
-                if item in items:
-                    slot = z_slot(sign, item)
-                    moved = lane_roll(load(item, yh), start - slot)
-                    block = moved if block is None else jnp.where(masks.z == slot, moved, block)
-        package[pl.ds(Z_BASE + yh * EDGE, EDGE), :] = block
+        for item in members(0, sign):
+            for yh in range(2):
+                package[pl.ds(x_row(item, sign, yh), 1), :] = a[item, yh, pl.ds(x_at, 1), :]
+        if fluid is not None:
+            for yh in range(2):
+                package[pl.ds(x_row(FLUID, sign, yh), 1), :] = fluid[yh, pl.ds(x_at, 1), :]
+    if fluid is not None:
+        package[pl.ds(YZ_FLUID, EDGE), :] = pack_axis(load, {key: FLUID for key in axis}, masks)
+
+
+def y_plane(ghost, direction, item, sign, at, masks, only=None):
+    if item in Y_NUMBER:
+        return lane_roll(ghost(direction, Y_ROWS, EDGE), Y_NUMBER[item] * EDGE - at)
+    block = ghost(direction, YZ_FLUID if item == FLUID else AXIS_ROWS, EDGE)
+    start = 4 * sign_index(sign) * EDGE + 4
+    first = lane_roll(block, start - at) if only is None or only < CUT else None
+    second = lane_roll(block, start + EDGE - CUT - at) if only is None or only >= CUT else None
+    if first is None or second is None:
+        return second if first is None else first
+    return jnp.where((masks.lane + (LANES - at)) % LANES < CUT, first, second)
+
+
+def z_plane(ghost, direction, item, sign, yh, target):
+    if item in Z_NUMBER:
+        return lane_roll(ghost(direction, Z_ROWS, EDGE), 2 * Z_NUMBER[item] + yh - target)
+    block = ghost(direction, YZ_FLUID if item == FLUID else AXIS_ROWS, EDGE)
+    return lane_roll(block, 2 * sign_index(sign) + yh - target)
 
 
 def pull(field, item, c, ghost, masks):
@@ -108,15 +166,13 @@
     v0, v1 = field
     if cx:
         edge = masks.row == (EDGE - 1 if cx == 1 else 0)
-        base = X_BASE[cx] + 2 * MEMBERS[(0, cx)].index(item)
-        v0 = jnp.where(edge, ghost((cx, 0, 0), base, 1), row_roll(v0, cx))
-        v1 = jnp.where(edge, ghost((cx, 0, 0), base + 1, 1), row_roll(v1, cx))
+        v0 = jnp.where(edge, ghost((cx, 0, 0), x_row(item, cx, 0), 1), row_roll(v0, cx))
+        v1 = jnp.where(edge, ghost((cx, 0, 0), x_row(item, cx, 1), 1), row_roll(v1, cx))
     if cy:
-        slot = MEMBERS[(1, cy)].index(item)
         at = 0 if cy == 1 else LANES - EDGE
-        plane = lane_roll(ghost((0, cy, 0), Y_BASE[cy], EDGE), slot * EDGE - at)
+        plane = y_plane(ghost, (0, cy, 0), item, cy, at, masks)
         if cx:
-            line = ghost((cx, cy, 0), base + (0 if cy == 1 else 1), 1)
+            line = ghost((cx, cy, 0), x_row(item, cx, 0 if cy == 1 else 1), 1)
             plane = jnp.where(edge, line, row_roll(plane, cx))
         if cy == 1:
             take = masks.lane < EDGE
@@ -127,18 +183,14 @@
         v0, v1 = lane_roll(v0, cy * EDGE), lane_roll(v1, cy * EDGE)
     if cz:
         target = EDGE - 1 if cz == 1 else 0
-        slot = z_slot(cz, item)
-        g = [lane_roll(ghost((0, 0, cz), Z_BASE + yh * EDGE, EDGE), slot - target) for yh in range(2)]
         source = EDGE - 1 - target
+        g = [z_plane(ghost, (0, 0, cz), item, cz, yh, target) for yh in range(2)]
         if cx:
             for yh in range(2):
-                line = lane_roll(ghost((cx, 0, cz), base + yh, 1), source - target)
+                line = lane_roll(ghost((cx, 0, cz), x_row(item, cx, yh), 1), source - target)
                 g[yh] = jnp.where(edge, line, row_roll(g[yh], cx))
         if cy:
-            line = lane_roll(
-                ghost((0, cy, cz), Y_BASE[cy], EDGE),
-                MEMBERS[(1, cy)].index(item) * EDGE + source - (at + target),
-            )
+            line = y_plane(ghost, (0, cy, cz), item, cy, at + target - source, masks, source)
             if cy == 1:
                 g = [jnp.where(take, g[1], g[0]), jnp.where(take, line, g[1])]
             else:
@@ -178,6 +230,9 @@
     return out
 
 
+AHEAD, BEHIND, SIBLING, PASSED = OWN + 2, OWN - 2, OWN + 1, OWN - 1
+
+
 def body(n, inner, *refs):
     (a_hbm, vel_hbm, relax_hbm, words, nbrs, ids, basis_hbm) = refs[:7]
     (out_hbm, grad) = refs[7:9]
@@ -188,15 +243,23 @@
     outer = n // inner
     place = me % inner
     group = me // inner
-    offsets = (2, -2, 1, -1)
-    halo_peers = [(me + d + n) % n for d in offsets]
+    way = 1 - 2 * (me % 2)
+    ahead, behind, sibling = me + 2 * way, me - 2 * way, me + way
+    has_ahead = (ahead >= 0) & (ahead < n)
+    has_behind = (behind >= 0) & (behind < n)
     inner_peers = [group * inner + (place + j) % inner for j in range(1, inner)]
     outer_peers = [((group + j) % outer) * inner + place for j in range(1, outer)]
-    peers = halo_peers + inner_peers + outer_peers
 
     barrier = pltpu.get_barrier_semaphore()
-    for peer in peers:
+
+    def greet(peer):
         pl.semaphore_signal(barrier, inc=1, device_id=(peer,), device_id_type=pl.DeviceIdType.MESH)
+
+    pl.when(has_ahead)(lambda: greet(ahead))
+    pl.when(has_behind)(lambda: greet(behind))
+    for peer in [sibling] + inner_peers + outer_peers:
+        greet(peer)
+    greetings = inner + outer - 1 + has_ahead.astype(jnp.int32) + has_behind.astype(jnp.int32)
 
     loads = []
     for yh in range(2):
@@ -232,44 +295,48 @@
     for k in range(NEIGHBOURS):
         entry = nbrs[0, k]
         there = (entry >= 0).astype(jnp.int32)
-        slot = jnp.clip(entry - me + OWN, 0, 2 * REACH)
+        slot = jnp.clip(OWN + (entry - me) * way, 0, 2 * REACH)
         slot_of.append(slot * there + OWN * (1 - there))
         present.append(there.astype(jnp.float32))
 
-    def send(step):
-        copies = []
-        for index, d in enumerate(offsets):
-            copies.append(
-                pltpu.make_async_remote_copy(
-                    src_ref=bufs[step].at[OWN],
-                    dst_ref=bufs[step].at[OWN - d],
-                    send_sem=send_sem.at[step, index],
-                    recv_sem=recv_sem.at[step, index],
-                    device_id=(halo_peers[index],),
-                    device_id_type=pl.DeviceIdType.MESH,
-                )
-            )
-        for copy in copies:
-            copy.start()
-        return copies
-
-    everything = set(range(1, VELS))
+    def halo(step, index, source, target, peer):
+        rows = pl.ds(0, ROWS if step == 0 else SENT)
+        return pltpu.make_async_remote_copy(
+            src_ref=bufs[step].at[source, rows],
+            dst_ref=bufs[step].at[target, rows],
+            send_sem=send_sem.at[step, index],
+            recv_sem=recv_sem.at[step, index],
+            device_id=(peer,),
+            device_id_type=pl.DeviceIdType.MESH,
+        )
+
+    def sum_copy(part, send, recv, j, peer):
+        return pltpu.make_async_remote_copy(
+            src_ref=part.at[pl.ds(0, 1)],
+            dst_ref=part.at[pl.ds(j, 1)],
+            send_sem=send.at[j - 1],
+            recv_sem=recv.at[j - 1],
+            device_id=(peer,),
+            device_id_type=pl.DeviceIdType.MESH,
+        )
+
     layer = [jnp.zeros((EDGE, LANES), jnp.float32) for _ in range(2)]
-
     for load in loads:
         load.wait()
+    exchanges = []
     for step in range(STEPS):
-        items = everything | ({FLUID} if step == 0 else set())
-        pack(
-            bufs[step].at[OWN],
-            lambda item, yh: fluid[yh] if item == FLUID else a[item, yh],
-            lambda item, yh, x: fluid[yh, pl.ds(x, 1), :] if item == FLUID else a[item, yh, pl.ds(x, 1), :],
-            items,
-            masks,
-        )
+        buf = bufs[step]
+        pack(buf.at[OWN], a, fluid if step == 0 else None, masks)
         if step == 0:
-            pl.semaphore_wait(barrier, len(peers))
-        copies = send(step)
+            pl.semaphore_wait(barrier, greetings)
+        to_ahead = halo(step, 0, OWN, BEHIND, ahead)
+        to_behind = halo(step, 1, OWN, AHEAD, behind)
+        to_sibling = halo(step, 2, OWN, SIBLING, sibling)
+        passing = halo(step, 3, AHEAD, PASSED, sibling)
+        exchanges.append((to_ahead, to_behind, to_sibling, passing))
+        pl.when(has_behind)(to_behind.start)
+        pl.when(has_ahead)(to_ahead.start)
+        to_sibling.start()
         for yh in range(2):
             layer[yh] = layer[yh] + (2.0 * a[5, yh] + ((a[11, yh] + a[14, yh]) + (a[15, yh] + a[18, yh])))
             if step == 0:
@@ -301,45 +368,27 @@
             for m in range(MODES):
                 product = jnp.sum(basis[m] * weight, axis=0, keepdims=True)
                 total = jnp.where(mode == m, product[:, :LANES] + product[:, LANES:], total)
-            part1[0] = total
-            sums1 = []
-            for j in range(1, inner):
-                sums1.append(
-                    pltpu.make_async_remote_copy(
-                        src_ref=part1.at[0],
-                        dst_ref=part1.at[j],
-                        send_sem=sum_send1.at[j - 1],
-                        recv_sem=sum_recv1.at[j - 1],
-                        device_id=(inner_peers[j - 1],),
-                        device_id_type=pl.DeviceIdType.MESH,
-                    )
-                )
+            total = jnp.sum(total, axis=1, keepdims=True)
+            at_mode = lax.broadcasted_iota(jnp.int32, (MODES, LANES), 1) == mode
+            part1[pl.ds(0, 1), :] = jnp.sum(jnp.where(at_mode, total, 0.0), axis=0, keepdims=True)
+            sums1 = [sum_copy(part1, sum_send1, sum_recv1, j, inner_peers[j - 1]) for j in range(1, inner)]
             for copy in sums1:
                 copy.start()
             for copy in sums1:
-                copy.wait()
-            total = part1[0]
-            for j in range(1, inner):
-                total = total + part1[j]
-            part2[0] = total
-            sums2 = []
-            for j in range(1, outer):
-                sums2.append(
-                    pltpu.make_async_remote_copy(
-                        src_ref=part2.at[0],
-                        dst_ref=part2.at[j],
-                        send_sem=sum_send2.at[j - 1],
-                        recv_sem=sum_recv2.at[j - 1],
-                        device_id=(outer_peers[j - 1],),
-                        device_id_type=pl.DeviceIdType.MESH,
-                    )
-                )
+                copy.wait_recv()
+            part2[pl.ds(0, 1), :] = jnp.sum(part1[...], axis=0, keepdims=True)
+            sums2 = [sum_copy(part2, sum_send2, sum_recv2, j, outer_peers[j - 1]) for j in range(1, outer)]
             for copy in sums2:
                 copy.start()
-        for copy in copies:
-            copy.wait()
-
-        buf = bufs[step]
+
+        @pl.when(has_ahead)
+        def _():
+            to_behind.wait_recv()
+            passing.start()
+
+        pl.when(has_behind)(to_ahead.wait_recv)
+        to_sibling.wait_recv()
+        pl.when(has_behind)(passing.wait_recv)
 
         def ghost(direction, row, rows):
             return buf[slot_of[DIRECTION[direction]], pl.ds(row, rows), :]
@@ -382,15 +431,15 @@
     for store in stores:
         store.start()
     for copy in sums2:
-        copy.wait()
-    total = part2[0]
-    for j in range(1, outer):
-        total = total + part2[j]
-    ones = jnp.ones((8, LANES), jnp.float32)
-    result = lax.dot_general(
-        ones, total, (((1,), (1,)), ((), ())), precision=lax.Precision.HIGHEST, preferred_element_type=jnp.float32
-    )
-    grad[...] = result[0:1, :]
+        copy.wait_recv()
+    grad[...] = jnp.sum(part2[...], axis=0, keepdims=True)[:, :MODES]
+    for to_ahead, to_behind, to_sibling, passing in exchanges:
+        pl.when(has_ahead)(to_ahead.wait_send)
+        pl.when(has_behind)(to_behind.wait_send)
+        to_sibling.wait_send()
+        pl.when(has_ahead)(passing.wait_send)
+    for copy in sums1 + sums2:
+        copy.wait_send()
     for store in stores:
         store.wait()
 
@@ -424,8 +473,8 @@
         ]
         + [pltpu.VMEM((2 * REACH + 1, ROWS, LANES), f32) for _ in range(STEPS)]
         + [
-            pltpu.VMEM((inner, MODES, LANES), f32),
-            pltpu.VMEM((outer, MODES, LANES), f32),
+            pltpu.VMEM((inner, LANES), f32),
+            pltpu.VMEM((outer, LANES), f32),
             dma((7,)),
             dma((STEPS, 4)),
             dma((STEPS, 4)),

time: 42.5 us -> 40.6 us (0.955)
  Pallas kernels: 39.4 us -> 37.4 us
    pallas_call x1, Pallas kernels: 39.4 us -> 37.4 us  [on_device(): pl.pallas_call(lambda *refs: body(n, inner, *refs), out_shape=(jax.ShapeD...]
where the time goes in v1:
time: 40.6 us; the launch traced here: 40.3 us
  Pallas kernels  37.4 us (92%)
  local copies, waits for them, and re-layouts  2.22 us (5%)
  between operations  0.65 us (2%)
    pallas_call x1, Pallas kernels, on_device(): pl.pallas_call(lambda *refs: body(n, inner, *refs), out_shape=(jax.ShapeD...  37.4 us
    unnamed x4, local copies, waits for them, and re-layouts  2.22 us

profile of v1, /device:TPU:1, one launch (start us, length us, event | category | flops | bytes accessed | tf_op | source)
XLA Modules:
  0.0 40.3 jit_solution(16010853807515978)
XLA Ops:
  0.6 37.4 %adjoint_steps.1 = (f32[19,16,2,128]{3,2,1,0:T(2,128)}, f32[1,8]{1,0:T(1,128)}) custom-call(f32[19,16,2,128]{3,2,1,0:T(2,128)} %bitcast.5, f32[3,16,2,128]{3,2,1,0:T(2,128)} %bitcast.7, f32[16,2,128]{2,1,0:T(2,128)} %bitcast.8, s32[1,128]{1,0:T(1,128)} %refs_3_.1, s32[1,18]{1,0:T(1,128)} %refs_4_.1, s32[16]{0:T(128)} %refs_5_.1, f32[8,16,256]{2,1,0:T(8,128)} %refs_6_.1), custom_call_target="tpu_custom_call" | custom-call | tf_op jit(solution)/shard_map/adjoint_steps/pallas_call | solution.py:456
  38.1 0.0 copy-start
  38.1 1.7 %copy.13 = f32[1,19,4096]{2,0,1:T(1,128)} copy(f32[1,19,4096]{2,0,1:T(1,128)} %bitcast.6) | data formatting | bytes 622592
  39.8 0.0 copy-done
  39.8 0.5 %copy.14 = f32[8]{0:T(128)} copy(f32[8]{0:T(128)S(1)} %bitcast.9) | data formatting | bytes 64
Async XLA Ops:
  38.1 1.7 %copy-start = (f32[1,8]{1,0:T(1,128)S(1)}, f32[1,8]{1,0:T(1,128)}, u32[]{:S(2)}) copy-start(f32[1,8]{1,0:T(1,128)} %get-tuple-element.5) | copy-start | bytes 100

commit v2 on v1

--- a/solution.py
+++ b/solution.py
@@ -161,45 +161,96 @@
     return lane_roll(block, 2 * sign_index(sign) + yh - target)
 
 
-def pull(field, item, c, ghost, masks):
+def inside(field, c, masks):
     cx, cy, cz = (int(v) for v in c)
     v0, v1 = field
     if cx:
-        edge = masks.row == (EDGE - 1 if cx == 1 else 0)
-        v0 = jnp.where(edge, ghost((cx, 0, 0), x_row(item, cx, 0), 1), row_roll(v0, cx))
-        v1 = jnp.where(edge, ghost((cx, 0, 0), x_row(item, cx, 1), 1), row_roll(v1, cx))
+        v0, v1 = row_roll(v0, cx), row_roll(v1, cx)
+    if cy == 1:
+        take = masks.lane < EDGE
+        v0, v1 = jnp.where(take, v1, v0), v1
+    elif cy == -1:
+        take = masks.lane >= LANES - EDGE
+        v0, v1 = v0, jnp.where(take, v0, v1)
+    by = cy * EDGE + cz
+    return lane_roll(v0, by), lane_roll(v1, by)
+
+
+def beyond(c, yh, masks):
+    cx, cy, cz = (int(v) for v in c)
+    out = None
+    if cx:
+        out = masks.row == (EDGE - 1 if cx == 1 else 0)
+    if cy and yh == (1 if cy == 1 else 0):
+        last = masks.yl == (LANES // EDGE - 1 if cy == 1 else 0)
+        out = last if out is None else out | last
+    if cz:
+        last = masks.z == (EDGE - 1 if cz == 1 else 0)
+        out = last if out is None else out | last
+    return out
+
+
+HALF = 8
+
+
+def outside(item, c, ghost, masks):
+    cx, cy, cz = (int(v) for v in c)
+    both = [(yh, half) for yh in range(2) for half in range(2)]
+
+    def part(value, half):
+        return value[HALF * half : HALF * (half + 1)]
+
+    if cx:
+        x_half = 1 if cx == 1 else 0
+        x_last = masks.row[:HALF] == (HALF - 1 if cx == 1 else 0)
+        x_line = [ghost((cx, 0, 0), x_row(item, cx, yh), 1) for yh in range(2)]
     if cy:
-        at = 0 if cy == 1 else LANES - EDGE
-        plane = y_plane(ghost, (0, cy, 0), item, cy, at, masks)
-        if cx:
-            line = ghost((cx, cy, 0), x_row(item, cx, 0 if cy == 1 else 1), 1)
-            plane = jnp.where(edge, line, row_roll(plane, cx))
-        if cy == 1:
-            take = masks.lane < EDGE
-            v0, v1 = jnp.where(take, v1, v0), jnp.where(take, plane, v1)
-        else:
-            take = masks.lane >= LANES - EDGE
-            v0, v1 = jnp.where(take, plane, v0), jnp.where(take, v0, v1)
-        v0, v1 = lane_roll(v0, cy * EDGE), lane_roll(v1, cy * EDGE)
+        y_half = 1 if cy == 1 else 0
+        at, final = (0, LANES - EDGE) if cy == 1 else (LANES - EDGE, 0)
+        plane = y_plane(ghost, (0, cy, 0), item, cy, final - cz, masks)
     if cz:
         target = EDGE - 1 if cz == 1 else 0
         source = EDGE - 1 - target
         g = [z_plane(ghost, (0, 0, cz), item, cz, yh, target) for yh in range(2)]
-        if cx:
-            for yh in range(2):
-                line = lane_roll(ghost((cx, 0, cz), x_row(item, cx, yh), 1), source - target)
-                g[yh] = jnp.where(edge, line, row_roll(g[yh], cx))
-        if cy:
-            line = y_plane(ghost, (0, cy, cz), item, cy, at + target - source, masks, source)
-            if cy == 1:
-                g = [jnp.where(take, g[1], g[0]), jnp.where(take, line, g[1])]
-            else:
-                g = [jnp.where(take, line, g[0]), jnp.where(take, g[0], g[1])]
-            g = [lane_roll(v, cy * EDGE) for v in g]
-        here = masks.z == target
-        v0 = jnp.where(here, g[0], lane_roll(v0, cz))
-        v1 = jnp.where(here, g[1], lane_roll(v1, cz))
-    return v0, v1
+    if cx and not cy and not cz:
+        return {(yh, x_half): jnp.broadcast_to(x_line[yh], (HALF, LANES)) for yh in range(2)}
+    if cy and not cx and not cz:
+        return {(y_half, half): part(plane, half) for half in range(2)}
+    if cz and not cx and not cy:
+        return {(yh, half): part(g[yh], half) for yh, half in both}
+    if cx and cy:
+        plane = row_roll(plane, cx)
+        line = ghost((cx, cy, 0), x_row(item, cx, 1 - y_half), 1)
+        lane = masks.lane[:1]
+        take = lane < EDGE if cy == 1 else lane >= LANES - EDGE
+        corner, other = (1, 0) if cy == 1 else (0, 1)
+        row = [None, None]
+        row[corner] = lane_roll(jnp.where(take, line, x_line[corner]), cy * EDGE)
+        row[other] = lane_roll(jnp.where(take, x_line[corner], x_line[other]), cy * EDGE)
+        return {
+            (other, x_half): jnp.broadcast_to(row[other], (HALF, LANES)),
+            (corner, x_half): jnp.where(x_last, row[corner], part(plane, x_half)),
+            (corner, 1 - x_half): part(plane, 1 - x_half),
+        }
+    if cx and cz:
+        found = {}
+        for yh in range(2):
+            line = lane_roll(ghost((cx, 0, cz), x_row(item, cx, yh), 1), source - target)
+            row = jnp.where(masks.z[:1] == target, line, lane_roll(x_line[yh], cz))
+            rolled = row_roll(g[yh], cx)
+            found[(yh, x_half)] = jnp.where(x_last, row, part(rolled, x_half))
+            found[(yh, 1 - x_half)] = part(rolled, 1 - x_half)
+        return found
+    line = y_plane(ghost, (0, cy, cz), item, cy, at + target - source, masks, source)
+    if cy == 1:
+        take = masks.lane < EDGE
+        g = [jnp.where(take, g[1], g[0]), jnp.where(take, line, g[1])]
+    else:
+        take = masks.lane >= LANES - EDGE
+        g = [jnp.where(take, line, g[0]), jnp.where(take, g[0], g[1])]
+    g = [lane_roll(v, cy * EDGE) for v in g]
+    g[y_half] = jnp.where(masks.z == target, g[y_half], plane)
+    return {(yh, half): part(g[yh], half) for yh, half in both}
 
 
 def collide(b, u, k, g, e):
@@ -230,21 +281,21 @@
     return out
 
 
-AHEAD, BEHIND, SIBLING, PASSED = OWN + 2, OWN - 2, OWN + 1, OWN - 1
+AHEAD, BEHIND, SIBLING, CROSS = OWN + 2, OWN - 2, OWN + 1, OWN - 1
 
 
 def body(n, inner, *refs):
     (a_hbm, vel_hbm, relax_hbm, words, nbrs, ids, basis_hbm) = refs[:7]
     (out_hbm, grad) = refs[7:9]
-    (a, b, vel, relax, basis, fluid, bits, coef) = refs[9:17]
-    bufs = refs[17 : 17 + STEPS]
-    (part1, part2, local_sem, send_sem, recv_sem, sum_send1, sum_recv1, sum_send2, sum_recv2) = refs[17 + STEPS :]
+    (a, b, vel, relax, basis, fluid, bits, coef, ghost_bits, spread) = refs[9:19]
+    bufs = refs[19 : 19 + STEPS]
+    (part1, part2, local_sem, send_sem, recv_sem, sum_send1, sum_recv1, sum_send2, sum_recv2) = refs[19 + STEPS :]
     me = lax.axis_index("blk")
     outer = n // inner
     place = me % inner
     group = me // inner
     way = 1 - 2 * (me % 2)
-    ahead, behind, sibling = me + 2 * way, me - 2 * way, me + way
+    ahead, behind, sibling, cross = me + 2 * way, me - 2 * way, me + way, me - way
     has_ahead = (ahead >= 0) & (ahead < n)
     has_behind = (behind >= 0) & (behind < n)
     inner_peers = [group * inner + (place + j) % inner for j in range(1, inner)]
@@ -257,16 +308,18 @@
 
     pl.when(has_ahead)(lambda: greet(ahead))
     pl.when(has_behind)(lambda: greet(behind))
+    pl.when(has_behind)(lambda: greet(cross))
     for peer in [sibling] + inner_peers + outer_peers:
         greet(peer)
-    greetings = inner + outer - 1 + has_ahead.astype(jnp.int32) + has_behind.astype(jnp.int32)
+    greetings = inner + outer - 1 + has_ahead.astype(jnp.int32) + 2 * has_behind.astype(jnp.int32)
 
     loads = []
     for yh in range(2):
         loads.append(pltpu.make_async_copy(a_hbm.at[:, :, yh, :], a.at[:, yh], local_sem.at[yh]))
         loads.append(pltpu.make_async_copy(vel_hbm.at[:, :, yh, :], vel.at[:, yh], local_sem.at[2 + yh]))
         loads.append(pltpu.make_async_copy(relax_hbm.at[:, yh, :], relax.at[yh], local_sem.at[4 + yh]))
-    loads.append(pltpu.make_async_copy(basis_hbm, basis, local_sem.at[6]))
+    load_basis = pltpu.make_async_copy(basis_hbm, basis, local_sem.at[6])
+    load_basis.start()
     for load in loads:
         load.start()
 
@@ -332,9 +385,10 @@
         to_ahead = halo(step, 0, OWN, BEHIND, ahead)
         to_behind = halo(step, 1, OWN, AHEAD, behind)
         to_sibling = halo(step, 2, OWN, SIBLING, sibling)
-        passing = halo(step, 3, AHEAD, PASSED, sibling)
-        exchanges.append((to_ahead, to_behind, to_sibling, passing))
+        to_cross = halo(step, 3, OWN, CROSS, cross)
+        exchanges.append((to_ahead, to_behind, to_sibling, to_cross))
         pl.when(has_behind)(to_behind.start)
+        pl.when(has_behind)(to_cross.start)
         pl.when(has_ahead)(to_ahead.start)
         to_sibling.start()
         for yh in range(2):
@@ -345,50 +399,66 @@
                 coef[0, yh] = f * (1.0 - relax[yh])
                 coef[1, yh] = f * relax[yh] * (1.0 / 12.0)
                 coef[2, yh] = (1.0 / 3.0) + 0.5 * squared
+        if step == 0:
+            load_basis.wait()
+            row = lax.broadcasted_iota(jnp.int32, (EDGE, 2 * LANES), 0)
+            flat = lax.broadcasted_iota(jnp.int32, (EDGE, 2 * LANES), 1)
+            mine = jnp.zeros((EDGE, 2 * LANES), jnp.float32)
+            for r in range(NIN):
+                mine = jnp.where(row == r, (ids[r] == me).astype(jnp.float32), mine)
+            lines = []
+            for m in range(MODES):
+                line = jnp.sum(basis[m] * mine, axis=0, keepdims=True)
+                lines.append(jnp.where(flat // EDGE == row, line, 0.0))
+            lines = jnp.concatenate(lines, axis=0)
+            q = lax.broadcasted_iota(jnp.int32, (2 * LANES, LANES), 0)
+            site = lax.broadcasted_iota(jnp.int32, (2 * LANES, LANES), 1)
+            for yh in range(2):
+                pick = ((site % EDGE == 0) & (site // EDGE + 8 * yh == q % EDGE)).astype(jnp.float32)
+                placed = jnp.dot(lines, pick, precision=lax.Precision.HIGHEST, preferred_element_type=jnp.float32)
+                for m in range(MODES):
+                    spread[m, yh] = placed[m * EDGE : (m + 1) * EDGE] * (fluid[yh] * (1.0 / 12.0))
         if step == STEPS - 1:
-            site = lax.broadcasted_iota(jnp.int32, (LANES, 2 * LANES), 0)
-            flat = lax.broadcasted_iota(jnp.int32, (LANES, 2 * LANES), 1)
-            spread = jnp.zeros((EDGE, 2 * LANES), jnp.float32)
-            for yh in range(2):
-                pick = ((site % EDGE == 0) & (site // EDGE + 8 * yh == flat % EDGE)).astype(jnp.float32)
-                value = jnp.where(masks.z == 0, layer[yh] * fluid[yh], 0.0) * (1.0 / 12.0)
-                spread = spread + jnp.dot(
-                    value, pick, precision=lax.Precision.HIGHEST, preferred_element_type=jnp.float32
-                )
-            row = lax.broadcasted_iota(jnp.int32, (EDGE, 2 * LANES), 0)
-            lane = lax.broadcasted_iota(jnp.int32, (EDGE, 2 * LANES), 1)
-            line = jnp.sum(jnp.where(lane // EDGE == row, spread, 0.0), axis=0, keepdims=True)
-            weight = jnp.zeros((EDGE, 2 * LANES), jnp.float32)
-            for r in range(NIN):
-                mine = (ids[r] == me).astype(jnp.float32)
-                weight = jnp.where(row == r, mine, weight)
-            weight = weight * line
             mode = lax.broadcasted_iota(jnp.int32, (MODES, LANES), 0)
             total = jnp.zeros((MODES, LANES), jnp.float32)
             for m in range(MODES):
-                product = jnp.sum(basis[m] * weight, axis=0, keepdims=True)
-                total = jnp.where(mode == m, product[:, :LANES] + product[:, LANES:], total)
+                product = spread[m, 0] * layer[0] + spread[m, 1] * layer[1]
+                total = jnp.where(mode == m, jnp.sum(product, axis=0, keepdims=True), total)
             total = jnp.sum(total, axis=1, keepdims=True)
             at_mode = lax.broadcasted_iota(jnp.int32, (MODES, LANES), 1) == mode
             part1[pl.ds(0, 1), :] = jnp.sum(jnp.where(at_mode, total, 0.0), axis=0, keepdims=True)
             sums1 = [sum_copy(part1, sum_send1, sum_recv1, j, inner_peers[j - 1]) for j in range(1, inner)]
             for copy in sums1:
                 copy.start()
+        for yh in range(2):
+            b[0, yh] = a[0, yh]
+        for i in range(1, VELS):
+            if step == 0:
+                moved = inside((fluid[0], fluid[1]), C[i], masks)
+                for yh in range(2):
+                    out = beyond(C[i], yh, masks)
+                    bits[i - 1, yh] = moved[yh] if out is None else jnp.where(out, 0.0, moved[yh])
+            moved = inside((a[i, 0], a[i, 1]), C[i], masks)
+            for yh in range(2):
+                back = a[OPP[i], yh]
+                if C[i][2] == -1:
+                    back = back * keep_z
+                b[i, yh] = jnp.where(bits[i - 1, yh] > 0.5, moved[yh], back)
+        if step == STEPS - 1:
             for copy in sums1:
                 copy.wait_recv()
             part2[pl.ds(0, 1), :] = jnp.sum(part1[...], axis=0, keepdims=True)
             sums2 = [sum_copy(part2, sum_send2, sum_recv2, j, outer_peers[j - 1]) for j in range(1, outer)]
             for copy in sums2:
                 copy.start()
-
-        @pl.when(has_ahead)
+        to_sibling.wait_recv()
+        pl.when(has_ahead)(to_behind.wait_recv)
+
+        @pl.when(has_behind)
         def _():
-            to_behind.wait_recv()
-            passing.start()
-
-        pl.when(has_behind)(to_ahead.wait_recv)
-        to_sibling.wait_recv()
-        pl.when(has_behind)(passing.wait_recv)
+            to_ahead.wait_recv()
+            to_cross.wait_recv()
+
 
         def ghost(direction, row, rows):
             return buf[slot_of[DIRECTION[direction]], pl.ds(row, rows), :]
@@ -400,21 +470,20 @@
                 return buf[slot_of[k], pl.ds(row, rows), :] * present[k]
 
             for i in range(1, VELS):
-                m0, m1 = pull((fluid[0], fluid[1]), FLUID, C[i], ghost_fluid, masks)
-                bits[i - 1, 0] = m0
-                bits[i - 1, 1] = m1
-        for yh in range(2):
-            b[0, yh] = a[0, yh]
+                for (yh, half), value in outside(FLUID, C[i], ghost_fluid, masks).items():
+                    rows = slice(HALF * half, HALF * (half + 1))
+                    value = jnp.where(beyond(C[i], yh, masks)[rows], value, 0.0)
+                    if C[i][2] == -1:
+                        value = value * keep_z[rows]
+                    ghost_bits[i - 1, yh, pl.ds(HALF * half, HALF), :] = value
         for i in range(1, VELS):
-            pulled = pull((a[i, 0], a[i, 1]), i, C[i], ghost, masks)
-            for yh in range(2):
-                value = jnp.where(bits[i - 1, yh] > 0.5, pulled[yh], a[OPP[i], yh])
-                if C[i][2] == -1:
-                    value = value * keep_z
-                b[i, yh] = value
+            for (yh, half), value in outside(i, C[i], ghost, masks).items():
+                rows = pl.ds(HALF * half, HALF)
+                b[i, yh, rows, :] = jnp.where(ghost_bits[i - 1, yh, rows, :] > 0.5, value, b[i, yh, rows, :])
+        stores = []
         for yh in range(2):
             for half in range(2):
-                rows = pl.ds(8 * half, 8)
+                rows = pl.ds(HALF * half, HALF)
                 new = collide(
                     [b[i, yh, rows, :] for i in range(VELS)],
                     [vel[c, yh, rows, :] for c in range(3)],
@@ -424,20 +493,21 @@
                 )
                 for i in range(VELS):
                     a[i, yh, rows, :] = new[i]
-
-    stores = [
-        pltpu.make_async_copy(a.at[:, yh], out_hbm.at[:, :, yh, :], local_sem.at[yh]) for yh in range(2)
-    ]
-    for store in stores:
-        store.start()
+                if step == STEPS - 1:
+                    store = pltpu.make_async_copy(
+                        a.at[:, yh, rows], out_hbm.at[:, rows, yh, :], local_sem.at[2 * yh + half]
+                    )
+                    store.start()
+                    stores.append(store)
+
     for copy in sums2:
         copy.wait_recv()
     grad[...] = jnp.sum(part2[...], axis=0, keepdims=True)[:, :MODES]
-    for to_ahead, to_behind, to_sibling, passing in exchanges:
+    for to_ahead, to_behind, to_sibling, to_cross in exchanges:
         pl.when(has_ahead)(to_ahead.wait_send)
         pl.when(has_behind)(to_behind.wait_send)
         to_sibling.wait_send()
-        pl.when(has_ahead)(passing.wait_send)
+        pl.when(has_behind)(to_cross.wait_send)
     for copy in sums1 + sums2:
         copy.wait_send()
     for store in stores:
@@ -470,6 +540,8 @@
             pltpu.VMEM((2, EDGE, LANES), f32),
             pltpu.VMEM((VELS - 1, 2, EDGE, LANES), f32),
             pltpu.VMEM((3, 2, EDGE, LANES), f32),
+            pltpu.VMEM((VELS - 1, 2, EDGE, LANES), f32),
+            pltpu.VMEM((MODES, 2, EDGE, LANES), f32),
         ]
         + [pltpu.VMEM((2 * REACH + 1, ROWS, LANES), f32) for _ in range(STEPS)]
         + [

time: 40.6 us -> 38.2 us (0.941)
  Pallas kernels: 37.4 us -> 35 us
    pallas_call x1, Pallas kernels: 37.4 us -> 35 us  [on_device(): pl.pallas_call(lambda *refs: body(n, inner, *refs), out_shape=(jax.ShapeD...]
where the time goes in v2:
time: 38.2 us; the launch traced here: 37.9 us
  Pallas kernels  35 us (92%)
  local copies, waits for them, and re-layouts  2.22 us (6%)
  between operations  0.65 us (2%)
    pallas_call x1, Pallas kernels, on_device(): pl.pallas_call(lambda *refs: body(n, inner, *refs), out_shape=(jax.ShapeD...  35 us
    unnamed x4, local copies, waits for them, and re-layouts  2.22 us

profile of v2, /device:TPU:1, one launch (start us, length us, event | category | flops | bytes accessed | tf_op | source)
XLA Modules:
  0.0 37.9 jit_solution(7876985476388309077)
XLA Ops:
  0.6 35.0 %adjoint_steps.1 = (f32[19,16,2,128]{3,2,1,0:T(2,128)}, f32[1,8]{1,0:T(1,128)}) custom-call(f32[19,16,2,128]{3,2,1,0:T(2,128)} %bitcast.5, f32[3,16,2,128]{3,2,1,0:T(2,128)} %bitcast.7, f32[16,2,128]{2,1,0:T(2,128)} %bitcast.8, s32[1,128]{1,0:T(1,128)} %refs_3_.1, s32[1,18]{1,0:T(1,128)} %refs_4_.1, s32[16]{0:T(128)} %refs_5_.1, f32[8,16,256]{2,1,0:T(8,128)} %refs_6_.1), custom_call_target="tpu_custom_call" | custom-call | tf_op jit(solution)/shard_map/adjoint_steps/pallas_call | solution.py:526
  35.7 0.0 copy-start
  35.7 1.7 %copy.13 = f32[1,19,4096]{2,0,1:T(1,128)} copy(f32[1,19,4096]{2,0,1:T(1,128)} %bitcast.6) | data formatting | bytes 622592
  37.4 0.0 copy-done
  37.4 0.5 %copy.14 = f32[8]{0:T(128)} copy(f32[8]{0:T(128)S(1)} %bitcast.9) | data formatting | bytes 64
Async XLA Ops:
  35.7 1.7 %copy-start = (f32[1,8]{1,0:T(1,128)S(1)}, f32[1,8]{1,0:T(1,128)}, u32[]{:S(2)}) copy-start(f32[1,8]{1,0:T(1,128)} %get-tuple-element.5) | copy-start | bytes 100

commit v3 on v2

--- a/solution.py
+++ b/solution.py
@@ -1,3 +1,5 @@
+import functools
+
 import jax
 import jax.numpy as jnp
 import numpy as np
@@ -286,10 +288,10 @@
 
 def body(n, inner, *refs):
     (a_hbm, vel_hbm, relax_hbm, words, nbrs, ids, basis_hbm) = refs[:7]
-    (out_hbm, grad) = refs[7:9]
-    (a, b, vel, relax, basis, fluid, bits, coef, ghost_bits, spread) = refs[9:19]
-    bufs = refs[19 : 19 + STEPS]
-    (part1, part2, local_sem, send_sem, recv_sem, sum_send1, sum_recv1, sum_send2, sum_recv2) = refs[19 + STEPS :]
+    (a, grad) = refs[7:9]
+    (b, vel, relax, basis, fluid, bits, coef, ghost_bits, spread) = refs[9:18]
+    bufs = refs[18 : 18 + STEPS]
+    (part1, part2, local_sem, send_sem, recv_sem, sum_send1, sum_recv1, sum_send2, sum_recv2) = refs[18 + STEPS :]
     me = lax.axis_index("blk")
     outer = n // inner
     place = me % inner
@@ -480,7 +482,6 @@
             for (yh, half), value in outside(i, C[i], ghost, masks).items():
                 rows = pl.ds(HALF * half, HALF)
                 b[i, yh, rows, :] = jnp.where(ghost_bits[i - 1, yh, rows, :] > 0.5, value, b[i, yh, rows, :])
-        stores = []
         for yh in range(2):
             for half in range(2):
                 rows = pl.ds(HALF * half, HALF)
@@ -493,12 +494,6 @@
                 )
                 for i in range(VELS):
                     a[i, yh, rows, :] = new[i]
-                if step == STEPS - 1:
-                    store = pltpu.make_async_copy(
-                        a.at[:, yh, rows], out_hbm.at[:, rows, yh, :], local_sem.at[2 * yh + half]
-                    )
-                    store.start()
-                    stores.append(store)
 
     for copy in sums2:
         copy.wait_recv()
@@ -510,6 +505,17 @@
         pl.when(has_behind)(to_cross.wait_send)
     for copy in sums1 + sums2:
         copy.wait_send()
+
+
+def hand_over(parts, state, grad_in, out, grad, sem):
+    stores = [pltpu.make_async_copy(grad_in, grad, sem.at[2 * parts])]
+    bounds = [VELS * j // parts for j in range(parts + 1)]
+    for j in range(parts):
+        for yh in range(2):
+            rows = pl.ds(bounds[j], bounds[j + 1] - bounds[j])
+            stores.append(pltpu.make_async_copy(state.at[rows, yh], out.at[rows, :, yh], sem.at[2 * j + yh]))
+    for store in stores:
+        store.start()
     for store in stores:
         store.wait()
 
@@ -526,13 +532,12 @@
     out, grad = pl.pallas_call(
         lambda *refs: body(n, inner, *refs),
         out_shape=(
-            jax.ShapeDtypeStruct((VELS,) + shape, f32),
+            pltpu.VMEM((VELS, 2, EDGE, LANES), f32),
             jax.ShapeDtypeStruct((1, MODES), f32),
         ),
         in_specs=[any_space, any_space, any_space, smem, smem, smem, any_space],
-        out_specs=(any_space, pl.BlockSpec(memory_space=pltpu.VMEM)),
+        out_specs=(pl.BlockSpec(memory_space=pltpu.VMEM), pl.BlockSpec(memory_space=pltpu.VMEM)),
         scratch_shapes=[
-            pltpu.VMEM((VELS, 2, EDGE, LANES), f32),
             pltpu.VMEM((VELS, 2, EDGE, LANES), f32),
             pltpu.VMEM((3, 2, EDGE, LANES), f32),
             pltpu.VMEM((2, EDGE, LANES), f32),
@@ -566,6 +571,18 @@
         inlet_ids,
         basis,
     )
+    parts = 4
+    out, grad = pl.pallas_call(
+        functools.partial(hand_over, parts),
+        out_shape=(
+            jax.ShapeDtypeStruct((VELS,) + shape, f32),
+            jax.ShapeDtypeStruct((1, MODES), f32),
+        ),
+        in_specs=[pl.BlockSpec(memory_space=pltpu.VMEM), any_space],
+        out_specs=(any_space, any_space),
+        scratch_shapes=[dma((2 * parts + 1,))],
+        name="hand_over",
+    )(pltpu.with_memory_space_constraint(out, pltpu.VMEM), grad)
     return (out.reshape(1, VELS, EDGE * EDGE * EDGE), grad.reshape(MODES))
 
 

time: 38.2 us -> 37.2 us (0.974)
  local copies, waits for them, and re-layouts: 2.22 us -> 0 us
  Pallas kernels: 35 us -> 36.3 us
    unnamed x4 -> x0, local copies, waits for them, and re-layouts: 2.22 us -> none
    pallas_call x1 -> x2, Pallas kernels: 35 us -> 36.3 us  [the longest x1 35.1 us: on_device(): pl.pallas_call(lambda *refs: body(n, inner, *refs), out_shape=(pltpu.VMEM...]
where the time goes in v3:
time: 37.2 us; the launch traced here: 36.9 us
  Pallas kernels  36.3 us (98%)
  between operations  0.64 us (2%)
    pallas_call x1, Pallas kernels, on_device(): pl.pallas_call(lambda *refs: body(n, inner, *refs), out_shape=(pltpu.VMEM...  35.1 us
    pallas_call x1, Pallas kernels, on_device(): pl.pallas_call(functools.partial(hand_over, parts), out_shape=(jax.ShapeD...  1.21 us

profile of v3, /device:TPU:1, one launch (start us, length us, event | category | flops | bytes accessed | tf_op | source)
XLA Modules:
  0.0 36.9 jit_solution(12075199056924815128)
XLA Ops:
  0.6 35.1 %adjoint_steps.1 = (f32[19,2,16,128]{3,2,1,0:T(8,128)S(1)}, f32[1,8]{1,0:T(1,128)}) custom-call(f32[19,16,2,128]{3,2,1,0:T(2,128)} %bitcast.5, f32[3,16,2,128]{3,2,1,0:T(2,128)} %bitcast.6, f32[16,2,128]{2,1,0:T(2,128)} %bitcast.7, s32[1,128]{1,0:T(1,128)} %refs_3_.1, s32[1,18]{1,0:T(1,128)} %refs_4_.1, s32[16]{0:T(128)} %refs_5_.1, f32[8,16,256]{2,1,0:T(8,128)} %refs_6_.1), custom_call_target="tpu_custom_call" | custom-call | tf_op jit(solution)/shard_map/adjoint_steps/pallas_call | solution.py:532
  35.7 1.2 %hand_over.1 = (f32[19,16,2,128]{3,2,1,0:T(2,128)}, f32[1,8]{1,0:T(1,128)}) custom-call(f32[19,2,16,128]{3,2,1,0:T(8,128)S(1)} %get-tuple-element.6.state, f32[1,8]{1,0:T(1,128)} %get-tuple-element.7.grad_in), custom_call_target="tpu_custom_call" | custom-call | tf_op jit(solution)/shard_map/hand_over/pallas_call | solution.py:575

commit v4 on v3

--- a/solution.py
+++ b/solution.py
@@ -287,11 +287,11 @@
 
 
 def body(n, inner, *refs):
-    (a_hbm, vel_hbm, relax_hbm, words, nbrs, ids, basis_hbm) = refs[:7]
+    (a_hbm, vel_hbm, relax_hbm, words_hbm, nbrs_hbm, ids_hbm, basis_hbm) = refs[:7]
     (a, grad) = refs[7:9]
-    (b, vel, relax, basis, fluid, bits, coef, ghost_bits, spread) = refs[9:18]
-    bufs = refs[18 : 18 + STEPS]
-    (part1, part2, local_sem, send_sem, recv_sem, sum_send1, sum_recv1, sum_send2, sum_recv2) = refs[18 + STEPS :]
+    (b, vel, relax, basis, fluid, bits, coef, ghost_bits, spread, words, nbrs, ids) = refs[9:21]
+    bufs = refs[21 : 21 + STEPS]
+    (part1, part2, local_sem, send_sem, recv_sem, sums1, sums2) = refs[21 + STEPS :]
     me = lax.axis_index("blk")
     outer = n // inner
     place = me % inner
@@ -300,8 +300,10 @@
     ahead, behind, sibling, cross = me + 2 * way, me - 2 * way, me + way, me - way
     has_ahead = (ahead >= 0) & (ahead < n)
     has_behind = (behind >= 0) & (behind < n)
-    inner_peers = [group * inner + (place + j) % inner for j in range(1, inner)]
-    outer_peers = [((group + j) % outer) * inner + place for j in range(1, outer)]
+    others = [t + (t >= place).astype(jnp.int32) for t in range(inner - 1)]
+    groups = [t + (t >= group).astype(jnp.int32) for t in range(outer - 1)]
+    inner_peers = [group * inner + p for p in others]
+    outer_peers = [g * inner + place for g in groups]
 
     barrier = pltpu.get_barrier_semaphore()
 
@@ -311,10 +313,16 @@
     pl.when(has_ahead)(lambda: greet(ahead))
     pl.when(has_behind)(lambda: greet(behind))
     pl.when(has_behind)(lambda: greet(cross))
-    for peer in [sibling] + inner_peers + outer_peers:
-        greet(peer)
+    greet(sibling)
     greetings = inner + outer - 1 + has_ahead.astype(jnp.int32) + 2 * has_behind.astype(jnp.int32)
 
+    tables = [
+        pltpu.make_async_copy(words_hbm, words, local_sem.at[7]),
+        pltpu.make_async_copy(nbrs_hbm, nbrs, local_sem.at[8]),
+        pltpu.make_async_copy(ids_hbm, ids, local_sem.at[9]),
+    ]
+    for table in tables:
+        table.start()
     loads = []
     for yh in range(2):
         loads.append(pltpu.make_async_copy(a_hbm.at[:, :, yh, :], a.at[:, yh], local_sem.at[yh]))
@@ -325,7 +333,12 @@
     for load in loads:
         load.start()
 
+    for peer in inner_peers + outer_peers:
+        greet(peer)
+
     masks = Masks()
+    for table in tables:
+        table.wait()
     for yh in range(2):
         word = jnp.zeros((EDGE, LANES), jnp.int32)
         for x in range(EDGE):
@@ -365,15 +378,21 @@
             device_id_type=pl.DeviceIdType.MESH,
         )
 
-    def sum_copy(part, send, recv, j, peer):
-        return pltpu.make_async_remote_copy(
-            src_ref=part.at[pl.ds(0, 1)],
-            dst_ref=part.at[pl.ds(j, 1)],
-            send_sem=send.at[j - 1],
-            recv_sem=recv.at[j - 1],
-            device_id=(peer,),
-            device_id_type=pl.DeviceIdType.MESH,
-        )
+    def start_sums(part, sems, mine, peers, places):
+        for peer, p in zip(peers, places):
+            row = 1 + mine - (mine > p).astype(jnp.int32)
+            pltpu.make_async_remote_copy(
+                src_ref=part.at[pl.ds(0, 1)],
+                dst_ref=part.at[pl.ds(row, 1)],
+                send_sem=sems.at[0],
+                recv_sem=sems.at[1],
+                device_id=(peer,),
+                device_id_type=pl.DeviceIdType.MESH,
+            ).start()
+
+    def wait_sums(part, sems, which):
+        rows = part.at[pl.ds(1, part.shape[0] - 1)]
+        pltpu.make_async_copy(rows, rows, sems.at[which]).wait()
 
     layer = [jnp.zeros((EDGE, LANES), jnp.float32) for _ in range(2)]
     for load in loads:
@@ -381,6 +400,18 @@
     exchanges = []
     for step in range(STEPS):
         buf = bufs[step]
+        for yh in range(2):
+            layer[yh] = layer[yh] + (2.0 * a[5, yh] + ((a[11, yh] + a[14, yh]) + (a[15, yh] + a[18, yh])))
+        if step == STEPS - 1:
+            mode = lax.broadcasted_iota(jnp.int32, (MODES, LANES), 0)
+            total = jnp.zeros((MODES, LANES), jnp.float32)
+            for m in range(MODES):
+                product = spread[m, 0] * layer[0] + spread[m, 1] * layer[1]
+                total = jnp.where(mode == m, jnp.sum(product, axis=0, keepdims=True), total)
+            total = jnp.sum(total, axis=1, keepdims=True)
+            at_mode = lax.broadcasted_iota(jnp.int32, (MODES, LANES), 1) == mode
+            part1[pl.ds(0, 1), :] = jnp.sum(jnp.where(at_mode, total, 0.0), axis=0, keepdims=True)
+            start_sums(part1, sums1, place, inner_peers, others)
         pack(buf.at[OWN], a, fluid if step == 0 else None, masks)
         if step == 0:
             pl.semaphore_wait(barrier, greetings)
@@ -394,7 +425,6 @@
         pl.when(has_ahead)(to_ahead.start)
         to_sibling.start()
         for yh in range(2):
-            layer[yh] = layer[yh] + (2.0 * a[5, yh] + ((a[11, yh] + a[14, yh]) + (a[15, yh] + a[18, yh])))
             if step == 0:
                 f = fluid[yh]
                 squared = vel[0, yh] * vel[0, yh] + vel[1, yh] * vel[1, yh] + vel[2, yh] * vel[2, yh]
@@ -420,18 +450,6 @@
                 placed = jnp.dot(lines, pick, precision=lax.Precision.HIGHEST, preferred_element_type=jnp.float32)
                 for m in range(MODES):
                     spread[m, yh] = placed[m * EDGE : (m + 1) * EDGE] * (fluid[yh] * (1.0 / 12.0))
-        if step == STEPS - 1:
-            mode = lax.broadcasted_iota(jnp.int32, (MODES, LANES), 0)
-            total = jnp.zeros((MODES, LANES), jnp.float32)
-            for m in range(MODES):
-                product = spread[m, 0] * layer[0] + spread[m, 1] * layer[1]
-                total = jnp.where(mode == m, jnp.sum(product, axis=0, keepdims=True), total)
-            total = jnp.sum(total, axis=1, keepdims=True)
-            at_mode = lax.broadcasted_iota(jnp.int32, (MODES, LANES), 1) == mode
-            part1[pl.ds(0, 1), :] = jnp.sum(jnp.where(at_mode, total, 0.0), axis=0, keepdims=True)
-            sums1 = [sum_copy(part1, sum_send1, sum_recv1, j, inner_peers[j - 1]) for j in range(1, inner)]
-            for copy in sums1:
-                copy.start()
         for yh in range(2):
             b[0, yh] = a[0, yh]
         for i in range(1, VELS):
@@ -447,12 +465,9 @@
                     back = back * keep_z
                 b[i, yh] = jnp.where(bits[i - 1, yh] > 0.5, moved[yh], back)
         if step == STEPS - 1:
-            for copy in sums1:
-                copy.wait_recv()
+            wait_sums(part1, sums1, 1)
             part2[pl.ds(0, 1), :] = jnp.sum(part1[...], axis=0, keepdims=True)
-            sums2 = [sum_copy(part2, sum_send2, sum_recv2, j, outer_peers[j - 1]) for j in range(1, outer)]
-            for copy in sums2:
-                copy.start()
+            start_sums(part2, sums2, group, outer_peers, groups)
         to_sibling.wait_recv()
         pl.when(has_ahead)(to_behind.wait_recv)
 
@@ -495,16 +510,15 @@
                 for i in range(VELS):
                     a[i, yh, rows, :] = new[i]
 
-    for copy in sums2:
-        copy.wait_recv()
+    wait_sums(part2, sums2, 1)
     grad[...] = jnp.sum(part2[...], axis=0, keepdims=True)[:, :MODES]
     for to_ahead, to_behind, to_sibling, to_cross in exchanges:
         pl.when(has_ahead)(to_ahead.wait_send)
         pl.when(has_behind)(to_behind.wait_send)
         to_sibling.wait_send()
         pl.when(has_behind)(to_cross.wait_send)
-    for copy in sums1 + sums2:
-        copy.wait_send()
+    wait_sums(part1, sums1, 0)
+    wait_sums(part2, sums2, 0)
 
 
 def hand_over(parts, state, grad_in, out, grad, sem):
@@ -527,7 +541,6 @@
     f32 = jnp.float32
     shape = (EDGE, 2, LANES)
     any_space = pl.BlockSpec(memory_space=pl.ANY)
-    smem = pl.BlockSpec(memory_space=pltpu.SMEM)
     dma = pltpu.SemaphoreType.DMA
     out, grad = pl.pallas_call(
         lambda *refs: body(n, inner, *refs),
@@ -535,7 +548,7 @@
             pltpu.VMEM((VELS, 2, EDGE, LANES), f32),
             jax.ShapeDtypeStruct((1, MODES), f32),
         ),
-        in_specs=[any_space, any_space, any_space, smem, smem, smem, any_space],
+        in_specs=[any_space] * 7,
         out_specs=(pl.BlockSpec(memory_space=pltpu.VMEM), pl.BlockSpec(memory_space=pltpu.VMEM)),
         scratch_shapes=[
             pltpu.VMEM((VELS, 2, EDGE, LANES), f32),
@@ -547,18 +560,19 @@
             pltpu.VMEM((3, 2, EDGE, LANES), f32),
             pltpu.VMEM((VELS - 1, 2, EDGE, LANES), f32),
             pltpu.VMEM((MODES, 2, EDGE, LANES), f32),
+            pltpu.SMEM((1, EDGE * EDGE * EDGE // 32), jnp.int32),
+            pltpu.SMEM((1, NEIGHBOURS), jnp.int32),
+            pltpu.SMEM((NIN,), jnp.int32),
         ]
         + [pltpu.VMEM((2 * REACH + 1, ROWS, LANES), f32) for _ in range(STEPS)]
         + [
             pltpu.VMEM((inner, LANES), f32),
             pltpu.VMEM((outer, LANES), f32),
-            dma((7,)),
+            dma((10,)),
             dma((STEPS, 4)),
             dma((STEPS, 4)),
-            dma((inner - 1,)),
-            dma((inner - 1,)),
-            dma((outer - 1,)),
-            dma((outer - 1,)),
+            dma((2,)),
+            dma((2,)),
         ],
         compiler_params=pltpu.CompilerParams(collective_id=0, has_side_effects=True),
         name="adjoint_steps",

time: 37.2 us -> 35.9 us (0.965)
  Pallas kernels: 36.3 us -> 35 us
    pallas_call x1, Pallas kernels: 35.1 us -> 33.8 us  [on_device(): pl.pallas_call(lambda *refs: body(n, inner, *refs), out_shape=(pltpu.VMEM...]
where the time goes in v4:
time: 35.9 us; the launch traced here: 35.7 us
  Pallas kernels  35 us (97%)
  between operations  0.64 us (2%)
    pallas_call x1, Pallas kernels, on_device(): pl.pallas_call(lambda *refs: body(n, inner, *refs), out_shape=(pltpu.VMEM...  33.8 us
    pallas_call x1, Pallas kernels, on_device(): pl.pallas_call(functools.partial(hand_over, parts), out_shape=(jax.ShapeD...  1.21 us

profile of v4, /device:TPU:1, one launch (start us, length us, event | category | flops | bytes accessed | tf_op | source)
XLA Modules:
  0.0 35.7 jit_solution(10971600663160616232)
XLA Ops:
  0.6 33.8 %adjoint_steps.1 = (f32[19,2,16,128]{3,2,1,0:T(8,128)S(1)}, f32[1,8]{1,0:T(1,128)}) custom-call(f32[19,16,2,128]{3,2,1,0:T(2,128)} %bitcast.5, f32[3,16,2,128]{3,2,1,0:T(2,128)} %bitcast.6, f32[16,2,128]{2,1,0:T(2,128)} %bitcast.7, s32[1,128]{1,0:T(1,128)} %refs_3_.1, s32[1,18]{1,0:T(1,128)} %refs_4_.1, s32[16]{0:T(128)} %refs_5_.1, f32[8,16,256]{2,1,0:T(8,128)} %refs_6_.1), custom_call_target="tpu_custom_call" | custom-call | tf_op jit(solution)/shard_map/adjoint_steps/pallas_call | solution.py:545
  34.5 1.2 %hand_over.1 = (f32[19,16,2,128]{3,2,1,0:T(2,128)}, f32[1,8]{1,0:T(1,128)}) custom-call(f32[19,2,16,128]{3,2,1,0:T(8,128)S(1)} %get-tuple-element.6.state, f32[1,8]{1,0:T(1,128)} %get-tuple-element.7.grad_in), custom_call_target="tpu_custom_call" | custom-call | tf_op jit(solution)/shard_map/hand_over/pallas_call | solution.py:589

commit v5 on v4

--- a/solution.py
+++ b/solution.py
@@ -420,9 +420,9 @@
         to_sibling = halo(step, 2, OWN, SIBLING, sibling)
         to_cross = halo(step, 3, OWN, CROSS, cross)
         exchanges.append((to_ahead, to_behind, to_sibling, to_cross))
+        pl.when(has_ahead)(to_ahead.start)
         pl.when(has_behind)(to_behind.start)
         pl.when(has_behind)(to_cross.start)
-        pl.when(has_ahead)(to_ahead.start)
         to_sibling.start()
         for yh in range(2):
             if step == 0:
@@ -546,7 +546,7 @@
         lambda *refs: body(n, inner, *refs),
         out_shape=(
             pltpu.VMEM((VELS, 2, EDGE, LANES), f32),
-            jax.ShapeDtypeStruct((1, MODES), f32),
+            pltpu.VMEM((1, MODES), f32),
         ),
         in_specs=[any_space] * 7,
         out_specs=(pl.BlockSpec(memory_space=pltpu.VMEM), pl.BlockSpec(memory_space=pltpu.VMEM)),
@@ -585,18 +585,18 @@
         inlet_ids,
         basis,
     )
-    parts = 4
+    parts = 1
     out, grad = pl.pallas_call(
         functools.partial(hand_over, parts),
         out_shape=(
             jax.ShapeDtypeStruct((VELS,) + shape, f32),
             jax.ShapeDtypeStruct((1, MODES), f32),
         ),
-        in_specs=[pl.BlockSpec(memory_space=pltpu.VMEM), any_space],
+        in_specs=[pl.BlockSpec(memory_space=pltpu.VMEM)] * 2,
         out_specs=(any_space, any_space),
         scratch_shapes=[dma((2 * parts + 1,))],
         name="hand_over",
-    )(pltpu.with_memory_space_constraint(out, pltpu.VMEM), grad)
+    )(pltpu.with_memory_space_constraint(out, pltpu.VMEM), pltpu.with_memory_space_constraint(grad, pltpu.VMEM))
     return (out.reshape(1, VELS, EDGE * EDGE * EDGE), grad.reshape(MODES))
 
 

time: 35.9 us -> 34.9 us (0.972)
  Pallas kernels: 35 us -> 34 us
    pallas_call x1, Pallas kernels: 33.8 us -> 33.3 us  [on_device(): pl.pallas_call(lambda *refs: body(n, inner, *refs), out_shape=(pltpu.VMEM...]
    pallas_call x1, Pallas kernels: 1.21 us -> 0.75 us  [on_device(): pl.pallas_call(functools.partial(hand_over, parts), out_shape=(jax.ShapeD...]
where the time goes in v5:
time: 34.9 us; the launch traced here: 34.7 us
  Pallas kernels  34 us (97%)
  between operations  0.64 us (2%)
    pallas_call x1, Pallas kernels, on_device(): pl.pallas_call(lambda *refs: body(n, inner, *refs), out_shape=(pltpu.VMEM...  33.3 us
    pallas_call x1, Pallas kernels, on_device(): pl.pallas_call(functools.partial(hand_over, parts), out_shape=(jax.ShapeD...  0.75 us

profile of v5, /device:TPU:1, one launch (start us, length us, event | category | flops | bytes accessed | tf_op | source)
XLA Modules:
  0.0 34.7 jit_solution(3437618864517631196)
XLA Ops:
  0.6 33.3 %adjoint_steps.1 = (f32[19,2,16,128]{3,2,1,0:T(8,128)S(1)}, f32[1,8]{1,0:T(1,128)S(1)}) custom-call(f32[19,16,2,128]{3,2,1,0:T(2,128)} %bitcast.5, f32[3,16,2,128]{3,2,1,0:T(2,128)} %bitcast.6, f32[16,2,128]{2,1,0:T(2,128)} %bitcast.7, s32[1,128]{1,0:T(1,128)} %refs_3_.1, s32[1,18]{1,0:T(1,128)} %refs_4_.1, s32[16]{0:T(128)} %refs_5_.1, f32[8,16,256]{2,1,0:T(8,128)} %refs_6_.1), custom_call_target="tpu_custom_call" | custom-call | tf_op jit(solution)/shard_map/adjoint_steps/pallas_call | solution.py:545
  33.9 0.7 %hand_over.1 = (f32[19,16,2,128]{3,2,1,0:T(2,128)}, f32[1,8]{1,0:T(1,128)}) custom-call(f32[19,2,16,128]{3,2,1,0:T(8,128)S(1)} %get-tuple-element.6.state, f32[1,8]{1,0:T(1,128)S(1)} %get-tuple-element.7.grad_in), custom_call_target="tpu_custom_call" | custom-call | tf_op jit(solution)/shard_map/hand_over/pallas_call | solution.py:589

commit v6 on v5

--- a/solution.py
+++ b/solution.py
@@ -291,7 +291,7 @@
     (a, grad) = refs[7:9]
     (b, vel, relax, basis, fluid, bits, coef, ghost_bits, spread, words, nbrs, ids) = refs[9:21]
     bufs = refs[21 : 21 + STEPS]
-    (part1, part2, local_sem, send_sem, recv_sem, sums1, sums2) = refs[21 + STEPS :]
+    (part1, part2, part3, without, local_sem, send_sem, recv_sem, sums1, sums2, direct) = refs[21 + STEPS :]
     me = lax.axis_index("blk")
     outer = n // inner
     place = me % inner
@@ -305,6 +305,17 @@
     inner_peers = [group * inner + p for p in others]
     outer_peers = [g * inner + place for g in groups]
 
+    apart = n // 4 // inner
+    late_groups = [apart * j - 1 for j in range(1, 4)] if apart > 2 else []
+    late = [g * inner + p for g in late_groups for p in (inner - 2, inner - 1)]
+    early_groups, early_places = range(2), inner // 2
+    early = [g * inner + p for g in early_groups for p in range(early_places)]
+    in_late_group = (group % apart == apart - 1) & (group < outer - 1) if late else False
+    is_late = in_late_group & (place >= inner - 2)
+    is_early = (group < 2) & (place < early_places)
+    is_split = in_late_group & (place < early_places)
+    is_top = (place >= inner - 2).astype(jnp.int32)
+
     barrier = pltpu.get_barrier_semaphore()
 
     def greet(peer):
@@ -314,7 +325,14 @@
     pl.when(has_behind)(lambda: greet(behind))
     pl.when(has_behind)(lambda: greet(cross))
     greet(sibling)
-    greetings = inner + outer - 1 + has_ahead.astype(jnp.int32) + 2 * has_behind.astype(jnp.int32)
+    if late:
+
+        @pl.when(is_early)
+        def _():
+            for device in late:
+                greet(device)
+
+    greetings = (len(early) * is_late.astype(jnp.int32) if late else 0) + inner + outer - 1 + has_ahead.astype(jnp.int32) + 2 * has_behind.astype(jnp.int32)
 
     tables = [
         pltpu.make_async_copy(words_hbm, words, local_sem.at[7]),
@@ -378,21 +396,32 @@
             device_id_type=pl.DeviceIdType.MESH,
         )
 
-    def start_sums(part, sems, mine, peers, places):
-        for peer, p in zip(peers, places):
-            row = 1 + mine - (mine > p).astype(jnp.int32)
-            pltpu.make_async_remote_copy(
-                src_ref=part.at[pl.ds(0, 1)],
-                dst_ref=part.at[pl.ds(row, 1)],
-                send_sem=sems.at[0],
-                recv_sem=sems.at[1],
-                device_id=(peer,),
-                device_id_type=pl.DeviceIdType.MESH,
-            ).start()
-
-    def wait_sums(part, sems, which):
-        rows = part.at[pl.ds(1, part.shape[0] - 1)]
-        pltpu.make_async_copy(rows, rows, sems.at[which]).wait()
+    def row_copy(source, target, row, sems, arrived, peer):
+        return pltpu.make_async_remote_copy(
+            src_ref=source,
+            dst_ref=target.at[pl.ds(row, 1)],
+            send_sem=sems.at[0],
+            recv_sem=sems.at[arrived],
+            device_id=(peer,),
+            device_id_type=pl.DeviceIdType.MESH,
+        )
+
+    def rank_at(mine, p):
+        return 1 + mine - (mine > p).astype(jnp.int32)
+
+    def wait_rows(part, sem, start, count):
+        rows = part.at[pl.ds(start, count)]
+        pltpu.make_async_copy(rows, rows, sem).wait()
+
+    def wait_first_stage(later):
+        for top, cut in ((0, inner - 2), (1, inner - 1)):
+
+            @pl.when(is_top == top)
+            def _(cut=cut):
+                if later:
+                    wait_rows(part1, sums1.at[2], cut, inner - cut)
+                else:
+                    wait_rows(part1, sums1.at[1], 1, cut - 1)
 
     layer = [jnp.zeros((EDGE, LANES), jnp.float32) for _ in range(2)]
     for load in loads:
@@ -411,7 +440,16 @@
             total = jnp.sum(total, axis=1, keepdims=True)
             at_mode = lax.broadcasted_iota(jnp.int32, (MODES, LANES), 1) == mode
             part1[pl.ds(0, 1), :] = jnp.sum(jnp.where(at_mode, total, 0.0), axis=0, keepdims=True)
-            start_sums(part1, sums1, place, inner_peers, others)
+            if late:
+
+                @pl.when(is_late)
+                def _():
+                    rank = 2 * (group // apart) + place - (inner - 2)
+                    for device in early:
+                        row_copy(part1.at[pl.ds(0, 1)], part3, rank, direct, 1, device).start()
+
+            for peer, p in zip(inner_peers, others):
+                row_copy(part1.at[pl.ds(0, 1)], part1, rank_at(place, p), sums1, 1 + is_top, peer).start()
         pack(buf.at[OWN], a, fluid if step == 0 else None, masks)
         if step == 0:
             pl.semaphore_wait(barrier, greetings)
@@ -465,9 +503,23 @@
                     back = back * keep_z
                 b[i, yh] = jnp.where(bits[i - 1, yh] > 0.5, moved[yh], back)
         if step == STEPS - 1:
-            wait_sums(part1, sums1, 1)
+            wait_first_stage(False)
+            if late:
+
+                @pl.when(is_split)
+                def _():
+                    without[...] = jnp.sum(part1[pl.ds(0, inner - 2), :], axis=0, keepdims=True)
+                    for g in early_groups:
+                        row_copy(without, part2, group, sums2, 1, g * inner + place).start()
+
+            wait_first_stage(True)
             part2[pl.ds(0, 1), :] = jnp.sum(part1[...], axis=0, keepdims=True)
-            start_sums(part2, sums2, group, outer_peers, groups)
+            for t, (peer, g) in enumerate(zip(outer_peers, groups)):
+                copy = row_copy(part2.at[pl.ds(0, 1)], part2, rank_at(group, g), sums2, 1, peer)
+                if late and t < len(early_groups):
+                    pl.when(jnp.logical_not(is_split))(copy.start)
+                else:
+                    copy.start()
         to_sibling.wait_recv()
         pl.when(has_ahead)(to_behind.wait_recv)
 
@@ -510,15 +562,23 @@
                 for i in range(VELS):
                     a[i, yh, rows, :] = new[i]
 
-    wait_sums(part2, sums2, 1)
-    grad[...] = jnp.sum(part2[...], axis=0, keepdims=True)[:, :MODES]
     for to_ahead, to_behind, to_sibling, to_cross in exchanges:
         pl.when(has_ahead)(to_ahead.wait_send)
         pl.when(has_behind)(to_behind.wait_send)
         to_sibling.wait_send()
         pl.when(has_behind)(to_cross.wait_send)
-    wait_sums(part1, sums1, 0)
-    wait_sums(part2, sums2, 0)
+    wait_rows(part1, sums1.at[0], 1, inner - 1)
+    wait_rows(part2, sums2.at[0], 1, outer - 1)
+    if late:
+        pl.when(is_late)(lambda: wait_rows(part3, direct.at[0], 0, len(early)))
+    wait_rows(part2, sums2.at[1], 1, outer - 1)
+    grad[...] = jnp.sum(part2[...], axis=0, keepdims=True)[:, :MODES]
+    if late:
+
+        @pl.when(is_early)
+        def _():
+            wait_rows(part3, direct.at[1], 0, len(late))
+            grad[...] += jnp.sum(part3[pl.ds(0, len(late)), :], axis=0, keepdims=True)[:, :MODES]
 
 
 def hand_over(parts, state, grad_in, out, grad, sem):
@@ -568,9 +628,12 @@
         + [
             pltpu.VMEM((inner, LANES), f32),
             pltpu.VMEM((outer, LANES), f32),
+            pltpu.VMEM((8, LANES), f32),
+            pltpu.VMEM((1, LANES), f32),
             dma((10,)),
             dma((STEPS, 4)),
             dma((STEPS, 4)),
+            dma((3,)),
             dma((2,)),
             dma((2,)),
         ],

time: 34.9 us -> 33.6 us (0.963)
  Pallas kernels: 34 us -> 32.8 us
    pallas_call x1, Pallas kernels: 33.3 us -> 32.1 us  [on_device(): pl.pallas_call(lambda *refs: body(n, inner, *refs), out_shape=(pltpu.VMEM...]
where the time goes in v6:
time: 33.6 us; the launch traced here: 33.5 us
  Pallas kernels  32.8 us (98%)
  between operations  0.64 us (2%)
    pallas_call x1, Pallas kernels, on_device(): pl.pallas_call(lambda *refs: body(n, inner, *refs), out_shape=(pltpu.VMEM...  32.1 us
    pallas_call x1, Pallas kernels, on_device(): pl.pallas_call(functools.partial(hand_over, parts), out_shape=(jax.ShapeD...  0.75 us

profile of v6, /device:TPU:1, one launch (start us, length us, event | category | flops | bytes accessed | tf_op | source)
XLA Modules:
  0.0 33.5 jit_solution(1610984627089646509)
XLA Ops:
  0.6 32.1 %adjoint_steps.1 = (f32[19,2,16,128]{3,2,1,0:T(8,128)S(1)}, f32[1,8]{1,0:T(1,128)S(1)}) custom-call(f32[19,16,2,128]{3,2,1,0:T(2,128)} %bitcast.5, f32[3,16,2,128]{3,2,1,0:T(2,128)} %bitcast.6, f32[16,2,128]{2,1,0:T(2,128)} %bitcast.7, s32[1,128]{1,0:T(1,128)} %refs_3_.1, s32[1,18]{1,0:T(1,128)} %refs_4_.1, s32[16]{0:T(128)} %refs_5_.1, f32[8,16,256]{2,1,0:T(8,128)} %refs_6_.1), custom_call_target="tpu_custom_call" | custom-call | tf_op jit(solution)/shard_map/adjoint_steps/pallas_call | solution.py:605
  32.7 0.7 %hand_over.1 = (f32[19,16,2,128]{3,2,1,0:T(2,128)}, f32[1,8]{1,0:T(1,128)}) custom-call(f32[19,2,16,128]{3,2,1,0:T(8,128)S(1)} %get-tuple-element.6.state, f32[1,8]{1,0:T(1,128)S(1)} %get-tuple-element.7.grad_in), custom_call_target="tpu_custom_call" | custom-call | tf_op jit(solution)/shard_map/hand_over/pallas_call | solution.py:652

commit v7 on v6

--- a/solution.py
+++ b/solution.py
@@ -52,8 +52,9 @@
     return sorted(found, key=lambda i: int(np.abs(C[i]).sum()), reverse=True)
 
 
-Z_ROWS, Y_ROWS, AXIS_ROWS, X_ROWS, X_FLUID, YZ_FLUID = 0, 16, 32, 48, 68, 72
-SENT, ROWS = 68, 88
+Z_ROWS, Y_ROWS, AXIS_ROWS, X_ROWS = 0, 16, 32, 48
+YZ_FLUID, X_FLUID = 0, 16
+ROWS, FLUID_ROWS = 68, 20
 SIGNS = (1, -1)
 Z_NUMBER = {i: n for n, i in enumerate([i for s in SIGNS for i in members(2, s)[:4]])}
 Y_NUMBER = {i: n for n, i in enumerate([i for s in SIGNS for i in members(1, s)[:4]])}
@@ -111,9 +112,20 @@
     return block
 
 
-def pack(package, a, fluid, masks):
+AXIS = {(1, 1): 3, (1, -1): 4, (2, 1): 5, (2, -1): 6}
+
+
+def pack_fluid(package, fluid, masks):
+    package[pl.ds(YZ_FLUID, EDGE), :] = pack_axis(lambda item, yh: fluid[yh], {key: FLUID for key in AXIS}, masks)
+    for sign in SIGNS:
+        for yh in range(2):
+            line = fluid[yh, pl.ds(0 if sign == 1 else EDGE - 1, 1), :]
+            package[pl.ds(x_row(FLUID, sign, yh), 1), :] = line
+
+
+def pack(package, a, masks):
     def load(item, yh):
-        return fluid[yh] if item == FLUID else a[item, yh]
+        return a[item, yh]
 
     block = None
     for sign in SIGNS:
@@ -130,18 +142,12 @@
             number = Y_NUMBER[item]
             block = put(block, masks.yl == number, lane_roll(load(item, yh), start - number * EDGE))
     package[pl.ds(Y_ROWS, EDGE), :] = block
-    axis = {(1, 1): 3, (1, -1): 4, (2, 1): 5, (2, -1): 6}
-    package[pl.ds(AXIS_ROWS, EDGE), :] = pack_axis(load, axis, masks)
+    package[pl.ds(AXIS_ROWS, EDGE), :] = pack_axis(load, AXIS, masks)
     for sign in SIGNS:
         x_at = 0 if sign == 1 else EDGE - 1
         for item in members(0, sign):
             for yh in range(2):
                 package[pl.ds(x_row(item, sign, yh), 1), :] = a[item, yh, pl.ds(x_at, 1), :]
-        if fluid is not None:
-            for yh in range(2):
-                package[pl.ds(x_row(FLUID, sign, yh), 1), :] = fluid[yh, pl.ds(x_at, 1), :]
-    if fluid is not None:
-        package[pl.ds(YZ_FLUID, EDGE), :] = pack_axis(load, {key: FLUID for key in axis}, masks)
 
 
 def y_plane(ghost, direction, item, sign, at, masks, only=None):
@@ -291,7 +297,7 @@
     (a, grad) = refs[7:9]
     (b, vel, relax, basis, fluid, bits, coef, ghost_bits, spread, words, nbrs, ids) = refs[9:21]
     bufs = refs[21 : 21 + STEPS]
-    (part1, part2, part3, without, local_sem, send_sem, recv_sem, sums1, sums2, direct) = refs[21 + STEPS :]
+    (fluids, part1, part2, part3, without, local_sem, send_sem, recv_sem, sums1, sums2, direct) = refs[21 + STEPS :]
     me = lax.axis_index("blk")
     outer = n // inner
     place = me % inner
@@ -308,11 +314,11 @@
     apart = n // 4 // inner
     late_groups = [apart * j - 1 for j in range(1, 4)] if apart > 2 else []
     late = [g * inner + p for g in late_groups for p in (inner - 2, inner - 1)]
-    early_groups, early_places = range(2), inner // 2
+    early_groups, early_places = range(3), inner - 2
     early = [g * inner + p for g in early_groups for p in range(early_places)]
     in_late_group = (group % apart == apart - 1) & (group < outer - 1) if late else False
     is_late = in_late_group & (place >= inner - 2)
-    is_early = (group < 2) & (place < early_places)
+    is_early = (group < len(early_groups)) & (place < early_places)
     is_split = in_late_group & (place < early_places)
     is_top = (place >= inner - 2).astype(jnp.int32)
 
@@ -386,10 +392,10 @@
         present.append(there.astype(jnp.float32))
 
     def halo(step, index, source, target, peer):
-        rows = pl.ds(0, ROWS if step == 0 else SENT)
+        buf = fluids if step == STEPS else bufs[step]
         return pltpu.make_async_remote_copy(
-            src_ref=bufs[step].at[source, rows],
-            dst_ref=bufs[step].at[target, rows],
+            src_ref=buf.at[source],
+            dst_ref=buf.at[target],
             send_sem=send_sem.at[step, index],
             recv_sem=recv_sem.at[step, index],
             device_id=(peer,),
@@ -426,6 +432,26 @@
     layer = [jnp.zeros((EDGE, LANES), jnp.float32) for _ in range(2)]
     for load in loads:
         load.wait()
+    def exchange(step):
+        to_ahead = halo(step, 0, OWN, BEHIND, ahead)
+        to_behind = halo(step, 1, OWN, AHEAD, behind)
+        to_sibling = halo(step, 2, OWN, SIBLING, sibling)
+        to_cross = halo(step, 3, OWN, CROSS, cross)
+        pl.when(has_ahead)(to_ahead.start)
+        pl.when(has_behind)(to_behind.start)
+        pl.when(has_behind)(to_cross.start)
+        to_sibling.start()
+        return (to_ahead, to_behind, to_sibling, to_cross)
+
+    def arrive(to_ahead, to_behind, to_sibling, to_cross):
+        to_sibling.wait_recv()
+        pl.when(has_ahead)(to_behind.wait_recv)
+
+        @pl.when(has_behind)
+        def _():
+            to_ahead.wait_recv()
+            to_cross.wait_recv()
+
     exchanges = []
     for step in range(STEPS):
         buf = bufs[step]
@@ -450,18 +476,12 @@
 
             for peer, p in zip(inner_peers, others):
                 row_copy(part1.at[pl.ds(0, 1)], part1, rank_at(place, p), sums1, 1 + is_top, peer).start()
-        pack(buf.at[OWN], a, fluid if step == 0 else None, masks)
+        pack(buf.at[OWN], a, masks)
         if step == 0:
+            pack_fluid(fluids.at[OWN], fluid, masks)
             pl.semaphore_wait(barrier, greetings)
-        to_ahead = halo(step, 0, OWN, BEHIND, ahead)
-        to_behind = halo(step, 1, OWN, AHEAD, behind)
-        to_sibling = halo(step, 2, OWN, SIBLING, sibling)
-        to_cross = halo(step, 3, OWN, CROSS, cross)
-        exchanges.append((to_ahead, to_behind, to_sibling, to_cross))
-        pl.when(has_ahead)(to_ahead.start)
-        pl.when(has_behind)(to_behind.start)
-        pl.when(has_behind)(to_cross.start)
-        to_sibling.start()
+            exchanges.append(exchange(STEPS))
+        exchanges.append(exchange(step))
         for yh in range(2):
             if step == 0:
                 f = fluid[yh]
@@ -520,23 +540,15 @@
                     pl.when(jnp.logical_not(is_split))(copy.start)
                 else:
                     copy.start()
-        to_sibling.wait_recv()
-        pl.when(has_ahead)(to_behind.wait_recv)
-
-        @pl.when(has_behind)
-        def _():
-            to_ahead.wait_recv()
-            to_cross.wait_recv()
-
-
         def ghost(direction, row, rows):
             return buf[slot_of[DIRECTION[direction]], pl.ds(row, rows), :]
 
         if step == 0:
+            arrive(*exchanges[0])
 
             def ghost_fluid(direction, row, rows):
                 k = DIRECTION[direction]
-                return buf[slot_of[k], pl.ds(row, rows), :] * present[k]
+                return fluids[slot_of[k], pl.ds(row, rows), :] * present[k]
 
             for i in range(1, VELS):
                 for (yh, half), value in outside(FLUID, C[i], ghost_fluid, masks).items():
@@ -545,6 +557,7 @@
                     if C[i][2] == -1:
                         value = value * keep_z[rows]
                     ghost_bits[i - 1, yh, pl.ds(HALF * half, HALF), :] = value
+        arrive(*exchanges[-1])
         for i in range(1, VELS):
             for (yh, half), value in outside(i, C[i], ghost, masks).items():
                 rows = pl.ds(HALF * half, HALF)
@@ -626,13 +639,14 @@
         ]
         + [pltpu.VMEM((2 * REACH + 1, ROWS, LANES), f32) for _ in range(STEPS)]
         + [
+            pltpu.VMEM((2 * REACH + 1, FLUID_ROWS, LANES), f32),
             pltpu.VMEM((inner, LANES), f32),
             pltpu.VMEM((outer, LANES), f32),
-            pltpu.VMEM((8, LANES), f32),
+            pltpu.VMEM((24, LANES), f32),
             pltpu.VMEM((1, LANES), f32),
             dma((10,)),
-            dma((STEPS, 4)),
-            dma((STEPS, 4)),
+            dma((STEPS + 1, 4)),
+            dma((STEPS + 1, 4)),
             dma((3,)),
             dma((2,)),
             dma((2,)),

time: 33.6 us -> 33.3 us (level)
  no operation moved by 1% of the time
where the time goes in v7:
time: 33.3 us; the launch traced here: 33.2 us
  Pallas kernels  32.5 us (98%)
  between operations  0.64 us (2%)
    pallas_call x1, Pallas kernels, on_device(): pl.pallas_call(lambda *refs: body(n, inner, *refs), out_shape=(pltpu.VMEM...  31.8 us
    pallas_call x1, Pallas kernels, on_device(): pl.pallas_call(functools.partial(hand_over, parts), out_shape=(jax.ShapeD...  0.75 us

profile of v7, /device:TPU:1, one launch (start us, length us, event | category | flops | bytes accessed | tf_op | source)
XLA Modules:
  0.0 33.2 jit_solution(15806840108361640899)
XLA Ops:
  0.6 31.8 %adjoint_steps.1 = (f32[19,2,16,128]{3,2,1,0:T(8,128)S(1)}, f32[1,8]{1,0:T(1,128)S(1)}) custom-call(f32[19,16,2,128]{3,2,1,0:T(2,128)} %bitcast.5, f32[3,16,2,128]{3,2,1,0:T(2,128)} %bitcast.6, f32[16,2,128]{2,1,0:T(2,128)} %bitcast.7, s32[1,128]{1,0:T(1,128)} %refs_3_.1, s32[1,18]{1,0:T(1,128)} %refs_4_.1, s32[16]{0:T(128)} %refs_5_.1, f32[8,16,256]{2,1,0:T(8,128)} %refs_6_.1), custom_call_target="tpu_custom_call" | custom-call | tf_op jit(solution)/shard_map/adjoint_steps/pallas_call | solution.py:618
  32.4 0.7 %hand_over.1 = (f32[19,16,2,128]{3,2,1,0:T(2,128)}, f32[1,8]{1,0:T(1,128)}) custom-call(f32[19,2,16,128]{3,2,1,0:T(8,128)S(1)} %get-tuple-element.6.state, f32[1,8]{1,0:T(1,128)S(1)} %get-tuple-element.7.grad_in), custom_call_target="tpu_custom_call" | custom-call | tf_op jit(solution)/shard_map/hand_over/pallas_call | solution.py:666

commit v8 on v7

--- a/solution.py
+++ b/solution.py
@@ -357,7 +357,7 @@
     for load in loads:
         load.start()
 
-    for peer in inner_peers + outer_peers:
+    for peer in outer_peers[::-1] + inner_peers:
         greet(peer)
 
     masks = Masks()
@@ -452,11 +452,15 @@
             to_ahead.wait_recv()
             to_cross.wait_recv()
 
+    def add_layer():
+        for yh in range(2):
+            layer[yh] = layer[yh] + (2.0 * a[5, yh] + ((a[11, yh] + a[14, yh]) + (a[15, yh] + a[18, yh])))
+
     exchanges = []
     for step in range(STEPS):
         buf = bufs[step]
-        for yh in range(2):
-            layer[yh] = layer[yh] + (2.0 * a[5, yh] + ((a[11, yh] + a[14, yh]) + (a[15, yh] + a[18, yh])))
+        if step == STEPS - 1:
+            add_layer()
         if step == STEPS - 1:
             mode = lax.broadcasted_iota(jnp.int32, (MODES, LANES), 0)
             total = jnp.zeros((MODES, LANES), jnp.float32)
@@ -482,6 +486,8 @@
             pl.semaphore_wait(barrier, greetings)
             exchanges.append(exchange(STEPS))
         exchanges.append(exchange(step))
+        if step < STEPS - 1:
+            add_layer()
         for yh in range(2):
             if step == 0:
                 f = fluid[yh]

time: 33.3 us -> 33.3 us (level)
  no operation moved by 1% of the time
where the time goes in v8:
time: 33.3 us; the launch traced here: 33.2 us
  Pallas kernels  32.5 us (98%)
  between operations  0.64 us (2%)
    pallas_call x1, Pallas kernels, on_device(): pl.pallas_call(lambda *refs: body(n, inner, *refs), out_shape=(pltpu.VMEM...  31.8 us
    pallas_call x1, Pallas kernels, on_device(): pl.pallas_call(functools.partial(hand_over, parts), out_shape=(jax.ShapeD...  0.75 us

profile of v8, /device:TPU:1, one launch (start us, length us, event | category | flops | bytes accessed | tf_op | source)
XLA Modules:
  0.0 33.2 jit_solution(14339887714532800950)
XLA Ops:
  0.6 31.8 %adjoint_steps.1 = (f32[19,2,16,128]{3,2,1,0:T(8,128)S(1)}, f32[1,8]{1,0:T(1,128)S(1)}) custom-call(f32[19,16,2,128]{3,2,1,0:T(2,128)} %bitcast.5, f32[3,16,2,128]{3,2,1,0:T(2,128)} %bitcast.6, f32[16,2,128]{2,1,0:T(2,128)} %bitcast.7, s32[1,128]{1,0:T(1,128)} %refs_3_.1, s32[1,18]{1,0:T(1,128)} %refs_4_.1, s32[16]{0:T(128)} %refs_5_.1, f32[8,16,256]{2,1,0:T(8,128)} %refs_6_.1), custom_call_target="tpu_custom_call" | custom-call | tf_op jit(solution)/shard_map/adjoint_steps/pallas_call | solution.py:624
  32.4 0.7 %hand_over.1 = (f32[19,16,2,128]{3,2,1,0:T(2,128)}, f32[1,8]{1,0:T(1,128)}) custom-call(f32[19,2,16,128]{3,2,1,0:T(8,128)S(1)} %get-tuple-element.6.state, f32[1,8]{1,0:T(1,128)S(1)} %get-tuple-element.7.grad_in), custom_call_target="tpu_custom_call" | custom-call | tf_op jit(solution)/shard_map/hand_over/pallas_call | solution.py:672

commit v9 on v8

--- a/solution.py
+++ b/solution.py
@@ -478,8 +478,6 @@
                     for device in early:
                         row_copy(part1.at[pl.ds(0, 1)], part3, rank, direct, 1, device).start()
 
-            for peer, p in zip(inner_peers, others):
-                row_copy(part1.at[pl.ds(0, 1)], part1, rank_at(place, p), sums1, 1 + is_top, peer).start()
         pack(buf.at[OWN], a, masks)
         if step == 0:
             pack_fluid(fluids.at[OWN], fluid, masks)
@@ -488,6 +486,9 @@
         exchanges.append(exchange(step))
         if step < STEPS - 1:
             add_layer()
+        else:
+            for peer, p in zip(inner_peers, others):
+                row_copy(part1.at[pl.ds(0, 1)], part1, rank_at(place, p), sums1, 1 + is_top, peer).start()
         for yh in range(2):
             if step == 0:
                 f = fluid[yh]

time: 33.3 us -> 33.3 us (level)
  no operation moved by 1% of the time
where the time goes in v9:
time: 33.3 us; the launch traced here: 33.2 us
  Pallas kernels  32.5 us (98%)
  between operations  0.64 us (2%)
    pallas_call x1, Pallas kernels, on_device(): pl.pallas_call(lambda *refs: body(n, inner, *refs), out_shape=(pltpu.VMEM...  31.8 us
    pallas_call x1, Pallas kernels, on_device(): pl.pallas_call(functools.partial(hand_over, parts), out_shape=(jax.ShapeD...  0.75 us

profile of v9, /device:TPU:1, one launch (start us, length us, event | category | flops | bytes accessed | tf_op | source)
XLA Modules:
  0.0 33.2 jit_solution(7982781040661083793)
XLA Ops:
  0.6 31.8 %adjoint_steps.1 = (f32[19,2,16,128]{3,2,1,0:T(8,128)S(1)}, f32[1,8]{1,0:T(1,128)S(1)}) custom-call(f32[19,16,2,128]{3,2,1,0:T(2,128)} %bitcast.5, f32[3,16,2,128]{3,2,1,0:T(2,128)} %bitcast.6, f32[16,2,128]{2,1,0:T(2,128)} %bitcast.7, s32[1,128]{1,0:T(1,128)} %refs_3_.1, s32[1,18]{1,0:T(1,128)} %refs_4_.1, s32[16]{0:T(128)} %refs_5_.1, f32[8,16,256]{2,1,0:T(8,128)} %refs_6_.1), custom_call_target="tpu_custom_call" | custom-call | tf_op jit(solution)/shard_map/adjoint_steps/pallas_call | solution.py:625
  32.4 0.7 %hand_over.1 = (f32[19,16,2,128]{3,2,1,0:T(2,128)}, f32[1,8]{1,0:T(1,128)}) custom-call(f32[19,2,16,128]{3,2,1,0:T(8,128)S(1)} %get-tuple-element.6.state, f32[1,8]{1,0:T(1,128)S(1)} %get-tuple-element.7.grad_in), custom_call_target="tpu_custom_call" | custom-call | tf_op jit(solution)/shard_map/hand_over/pallas_call | solution.py:673
